TPU v7x, 32 devices: a whole 2x2x4 slice. The times are simulated.
32 devices in a mesh: depth: 2 (over x), gx: 8 (over z, y), gy: 2 (over core).
Axes of the slice: x: 2, y: 2, z: 4, core: 2. Of those that a mesh axis runs over, the one named last changes fastest.
Arguments:
- operator: bfloat16 [2, 8, 2, 1536, 1536], P('depth', 'gx', 'gy')
- sources: bfloat16 [2, 8, 2, 768, 1024], P('depth', 'gx', 'gy'), may hold values from -6 to 6
Outputs:
- solution: bfloat16 [2, 8, 2, 768, 1024], P('depth', 'gx', 'gy')
All inputs are finite; a program needn't handle non-finite values.
Results may differ from a plain program's by a relative error of at most 0.017.
Values may be sent and summed in bfloat16 or wider, within the bound.
No kernel may reach another device: no remote copies, remote signals or barrier semaphores. Data moves between devices by JAX's collectives and lax.ppermute only.
A program may use at most 64 MiB of HBM per device.

v0:
```python
import functools
import jax
import jax.numpy as jnp
from jax import lax
from jax.experimental import pallas as pl
from jax.experimental.pallas import tpu as pltpu
from jax.sharding import PartitionSpec as P

STREAMS = 4
BLOCKS = 2
REPEAT = (8, 4, 4)
VMEM = pl.BlockSpec(memory_space=pltpu.VMEM)
SMEM = pl.BlockSpec(memory_space=pltpu.SMEM)
HBM = pl.BlockSpec(memory_space=pltpu.HBM)
AXES = ("depth", "gx", "gy")
f32 = jnp.float32
bf16 = jnp.bfloat16


def dot(a, b):
    return jnp.dot(a, b, preferred_element_type=f32)


def shaped(shape, dtype=bf16):
    return jax.ShapeDtypeStruct(shape, dtype)


def call(kernel, ins, outs, out_specs, mib, flops, nbytes, scratch=(), aliases=None):
    return pl.pallas_call(
        kernel,
        out_shape=outs,
        in_specs=ins,
        out_specs=out_specs,
        scratch_shapes=list(scratch),
        input_output_aliases=aliases or {},
        compiler_params=pltpu.CompilerParams(vmem_limit_bytes=mib << 20),
        cost_estimate=pl.CostEstimate(flops=flops, bytes_accessed=nbytes, transcendentals=0),
    )


def route(sizes, axis, tick):
    nd, nx, ny = sizes
    pairs = []
    for d in range(nd):
        for i in range(nx):
            for j in range(ny):
                group = j // 2
                at, to = [d, i, group], [d, i, group]
                to[axis] += 1
                if to[axis] < (nd, nx, ny // 2)[axis] and (sum(at) - tick) % REPEAT[axis] == 0:
                    end = (to[0] * nx + to[1]) * ny + 2 * to[2] + j % 2
                    pairs.append(((d * nx + i) * ny + j, end))
    return pairs


def fetch_kernel(trace, op_ref, turn_ref, mid_ref, rest_ref):
    del turn_ref
    mid_ref[...] = op_ref[:, trace : 2 * trace]
    rest_ref[:, :trace] = op_ref[:, :trace]
    rest_ref[:, trace:] = op_ref[:, 2 * trace : 3 * trace]


def give_kernel(half, parity_ref, op_ref, src_ref, turn_ref, give_ref):
    del turn_ref
    columns = pl.ds(pl.multiple_of((1 - parity_ref[0]) * half, 128), half)
    rows = op_ref.shape[0]
    give_ref[...] = dot(op_ref[:, rows:], src_ref[:, columns]).astype(bf16)


def half_kernel(half, parity_ref, op_ref, src_ref, turn_ref, out_ref):
    del turn_ref
    columns = pl.ds(pl.multiple_of(parity_ref[0] * half, 128), half)
    rows = out_ref.shape[0]
    step = rows // 3

    def body(n, _):
        part = pl.ds(pl.multiple_of(n * step, step), step)
        out_ref[part, :] = dot(op_ref[part, rows:], src_ref[:, columns])
        return 0

    lax.fori_loop(0, 3, body, 0)


def both_kernel(parity_ref, op_ref, mid_ref, turn_ref, *refs):
    del turn_ref
    *rest, both_ref = refs
    trace = mid_ref.shape[1]
    own, other = parity_ref[0], 1 - parity_ref[0]
    both_ref[own, :, trace : 2 * trace] = op_ref[:, trace : 2 * trace]
    both_ref[other, :, trace : 2 * trace] = mid_ref[...]
    for rest_ref in rest:
        both_ref[own, :, :trace] = op_ref[:, :trace]
        both_ref[own, :, 2 * trace :] = op_ref[:, 2 * trace : 3 * trace]
        both_ref[other, :, :trace] = rest_ref[:, :trace]
        both_ref[other, :, 2 * trace :] = rest_ref[:, trace:]


def lower_kernel(rows, op_ref, src_ref, turn_ref, r_ref, token_ref):
    del turn_ref
    step = r_ref.shape[0] // 3
    token_ref[...] = jnp.zeros(token_ref.shape, token_ref.dtype)

    def body(n, _):
        part = pl.ds(pl.multiple_of(n * step, step), step)
        below = pl.ds(pl.multiple_of(rows + n * step, step), step)
        r_ref[part, :] = dot(op_ref[below, rows:], src_ref[...])
        return 0

    lax.fori_loop(0, 3, body, 0)


def pair_sources(parity_ref, s_ref, given_ref, rows, columns):
    own, given = s_ref[rows, columns], given_ref[rows, columns].astype(f32)
    even = parity_ref[0] == 0
    return jnp.where(even, own, given), jnp.where(even, given, own)


def lower_side(op, rows, trace, total, parts):
    for n, part in enumerate(parts):
        if part is not None:
            total += dot(op[rows, n * trace : (n + 1) * trace], part)
    return total


def halves(ref, trace):
    return (None, None) if ref is None else (ref[:trace, :], ref[trace:, :])


def paired(ref, trace, slot):
    if ref is None:
        return None, None
    at = 2 * slot * trace
    return ref[at : at + trace, :], ref[at + trace : at + 2 * trace, :]


def tick_kernel(tick, trace, columns, slot, moving, has_row, level_ref, parity_ref, both_ref, s_ref, given_ref, turn_ref, *refs):
    del turn_ref
    refs = list(refs)
    x_in = refs.pop(0) if moving else None
    z_in = refs.pop(0) if moving else None
    y_in = refs.pop(0) if moving and has_row else None
    x_out, mid_out = refs[:2]

    @pl.when(level_ref[0] == tick)
    def _():
        xa, xb = halves(x_in, trace)
        za, zb = paired(z_in, trace, slot)
        ya = None if y_in is None else y_in[...]
        upper = slice(0, 2 * trace)
        sa, sb = pair_sources(parity_ref, s_ref, given_ref, upper, columns)
        a = lower_side(both_ref.at[0], upper, trace, sa, (xa, ya, za)).astype(bf16)
        mid = a[trace:]
        wanted = slice(0, (1 + has_row) * trace)
        b = lower_side(both_ref.at[1], wanted, trace, sb[wanted], (xb, None, zb))
        b = lower_side(both_ref.at[1], wanted, trace, b, (None, mid, None)).astype(bf16)
        x_out[:trace, :] = a[:trace]
        x_out[trace:, :] = b[:trace]
        mid_out[...] = mid
        if has_row:
            refs[2][...] = b[trace:]


def depth_kernel(tick, trace, columns, moving, has_row, level_ref, parity_ref, more_ref, both_ref, s_ref, given_ref, *refs):
    refs = list(refs)
    xs = [refs.pop(0) for _ in range(2)] if moving else [None] * 2
    z_in = refs.pop(0) if moving else None
    ys = [refs.pop(0) for _ in range(2)] if moving and has_row else [None] * 2
    mids = [refs.pop(0) for _ in range(2)]
    z_out = refs[0]
    width = z_out.shape[1]

    @pl.when(jnp.logical_and(level_ref[0] == tick, more_ref[0] == 1))
    def _():
        rows = slice(2 * trace, 3 * trace)

        def side_by_side(parts):
            return None if parts[0] is None else jnp.concatenate(parts, axis=1)

        pairs = [halves(ref, trace) + paired(z_in, trace, slot) for slot, ref in enumerate(xs)]
        xa, xb, za, zb = [side_by_side(parts) for parts in zip(*pairs)]
        ya = side_by_side([None if ref is None else ref[...] for ref in ys])
        mid = side_by_side([ref[...] for ref in mids])
        sa, sb = pair_sources(parity_ref, s_ref, given_ref, rows, columns)
        a = lower_side(both_ref.at[0], rows, trace, sa, (xa, ya, za)).astype(bf16)
        b = lower_side(both_ref.at[1], rows, trace, sb, (xb, mid, zb)).astype(bf16)
        for slot in range(2):
            part = slice(slot * width, (slot + 1) * width)
            z_out[2 * slot * trace : (2 * slot + 1) * trace, :] = a[:, part]
            z_out[(2 * slot + 1) * trace : (2 * slot + 2) * trace, :] = b[:, part]


def last_kernel(top, trace, width, base, has_row, level_ref, parity_ref, both_ref, s_ref, given_ref, turn_ref, *refs):
    del turn_ref
    refs = list(refs)
    own_ref, give_ref = refs[-2:]
    even = parity_ref[0] == 0
    zero = jnp.zeros((trace, width), bf16)

    def put(n, slot, a, b):
        rows = slice(n * trace, (n + 1) * trace)
        cols = slice(slot * width, (slot + 1) * width)
        own_ref[rows, cols] = jnp.where(even, a, b)
        give_ref[rows, cols] = jnp.where(even, b, a)

    for tick in range(top + 1):
        z_in = refs.pop(0) if tick else None
        xs = [refs.pop(0) for _ in range(2)] if tick else [None] * 2
        ys = [refs.pop(0) for _ in range(2)] if tick and has_row else [None] * 2
        mids = [refs.pop(0) for _ in range(2)] if tick < top else [None] * 2

        @pl.when(level_ref[0] == tick)
        def _():
            for slot in range(2):
                xa, xb = halves(xs[slot], trace)
                za, zb = paired(z_in, trace, slot)
                ya = None if ys[slot] is None else ys[slot][...]
                if mids[slot] is None:
                    rows = slice(trace, 2 * trace)
                    start = base + slot * width
                    sa, _ = pair_sources(parity_ref, s_ref, given_ref, rows, slice(start, start + width))
                    yb = lower_side(both_ref.at[0], rows, trace, sa, (xa, ya, za)).astype(bf16)
                else:
                    yb = mids[slot][...]
                put(0, slot, zero if xa is None else xa, zero if xb is None else xb)
                put(1, slot, zero if ya is None else ya, yb)
                put(2, slot, zero if za is None else za, zero if zb is None else zb)


def solved(columns, op_ref, r_ref, in_ref, start=0, stop=None):
    rows = in_ref.shape[0]
    stop = r_ref.shape[0] if stop is None else stop
    return (r_ref[start:stop, columns] + dot(op_ref[rows + start : rows + stop, :rows], in_ref[...])).astype(bf16)


def solve_kernel(half, base, side, parity_ref, op_ref, r_ref, in_ref, turn_ref, out_ref, token_ref):
    del turn_ref
    at = parity_ref[0] if side == 0 else 1 - parity_ref[0]
    columns = pl.ds(pl.multiple_of(at * half + base, 128), out_ref.shape[1])
    token_ref[...] = jnp.zeros(token_ref.shape, token_ref.dtype)
    out_ref[...] = solved(columns, op_ref, r_ref, in_ref)


def final_kernel(half, parity_ref, op_ref, r_ref, in_ref, turn_ref, *refs):
    del turn_ref
    *pieces, out_ref, buf, sems = refs
    width = in_ref.shape[1]
    blocks = sems.shape[0]
    step = buf.shape[0] // blocks

    def columns(n):
        at = parity_ref[0] if n % 2 == 0 else 1 - parity_ref[0]
        return pl.ds(pl.multiple_of(at * half + n // 2 * width, 128), width)

    copies = []
    for n in range(blocks):
        part = slice(n * step, (n + 1) * step)
        last = columns(len(pieces))
        buf[part, last] = solved(last, op_ref, r_ref, in_ref, n * step, (n + 1) * step)
        for k, piece in enumerate(pieces):
            buf[part, columns(k)] = piece[part, :]
        rows = pl.ds(n * step, step)
        copies.append(pltpu.make_async_copy(buf.at[rows, :], out_ref.at[rows, :], sems.at[n]))
        copies[-1].start()
    for copy in copies:
        copy.wait()


def shards(sizes, operator, sources):
    op = operator[0, 0, 0]
    src = sources[0, 0, 0]
    inner, columns = src.shape
    trace = (op.shape[0] - inner) // 3
    rows = 3 * trace
    half = columns // 2
    width = half // STREAMS
    nd, nx, ny = sizes
    top = nd + nx + ny // 2 - 3
    has_row = ny > 2
    row = lax.axis_index("gy")
    level = lax.axis_index("depth") + lax.axis_index("gx") + (row >> 1)
    level = level.astype(jnp.int32).reshape(1)
    parity = (row & 1).astype(jnp.int32).reshape(1)
    more = (lax.axis_index("depth") < nd - 1).astype(jnp.int32).reshape(1)
    op, src, level, parity, more = lax.optimization_barrier((op, src, level, parity, more))
    swap = [(j, j ^ 1) for j in range(ny)]

    upper = op[:rows]
    mid, rest = call(
        functools.partial(fetch_kernel, trace), [VMEM] * 2,
        [shaped((rows, trace)), shaped((rows, 2 * trace))], [VMEM] * 2, 4, 0, 0,
    )(upper, src)
    mid_got = lax.ppermute(mid, "gy", swap)
    give = call(
        functools.partial(give_kernel, half), [SMEM] + [VMEM] * 3, shaped((rows, half)), VMEM, 4, 0, 0
    )(parity, upper, src, mid)
    given = lax.ppermute(give, "gy", swap)
    rest_got = lax.ppermute(rest, "gy", swap)
    s = call(
        functools.partial(half_kernel, half), [SMEM] + [VMEM] * 3, shaped((rows, half), f32), VMEM, 4, 0, 0
    )(parity, upper, src, give)

    def joined(after, *parts):
        return call(both_kernel, [SMEM] + [VMEM] * (3 + len(parts)), shaped((2, rows, rows)), VMEM, 4, 0, 0)(
            parity, upper, mid_got, after, *parts
        )

    both = joined(s)
    turn = given
    xs = [[] for _ in range(STREAMS)]
    ys = [[] for _ in range(STREAMS)]
    zs = [[] for _ in range(STREAMS // 2)]
    mids = [[] for _ in range(STREAMS)]
    for tick in range(top):
        for n in range(STREAMS):
            slot = n % 2
            cols = slice(n * width, (n + 1) * width)
            outs = [shaped((2 * trace, width)), shaped((trace, width))] + [shaped((trace, width))] * has_row
            ins = [turn]
            if tick:
                ins += [xs[n][-1], zs[n // 2][tick - 1]] + ([ys[n][-1]] if has_row else [])
            sent = call(
                functools.partial(tick_kernel, tick, trace, cols, slot, tick > 0, has_row),
                [SMEM] * 2 + [VMEM] * (3 + len(ins)), outs, [VMEM] * len(outs), 4, 0, 0,
            )(level, parity, both, s, given, *ins)
            turn = sent[1]
            mids[n].append(turn)
            xs[n].append(lax.ppermute(sent[0], AXES, route(sizes, 1, tick)))
            if has_row:
                ys[n].append(lax.ppermute(sent[2], AXES, route(sizes, 2, tick)))
            if slot:
                both_slots = (n - 1, n)
                ins = []
                if tick:
                    ins += [xs[m][tick - 1] for m in both_slots] + [zs[n // 2][tick - 1]]
                    ins += [ys[m][tick - 1] for m in both_slots] if has_row else []
                ins += [mids[m][tick] for m in both_slots]
                cols = slice((n - 1) * width, (n + 1) * width)
                turn = call(
                    functools.partial(depth_kernel, tick, trace, cols, tick > 0, has_row),
                    [SMEM] * 3 + [VMEM] * (3 + len(ins)), shaped((4 * trace, width)), VMEM, 4, 0, 0,
                )(level, parity, more, both, s, given, *ins)
                zs[n // 2].append(lax.ppermute(turn, AXES, route(sizes, 0, tick)))
        if tick == 0:
            both = turn = joined(turn, rest_got)
        if tick == top // 2:
            r, turn = call(
                functools.partial(lower_kernel, rows), [VMEM] * 3,
                [shaped((inner, columns), f32), shaped((8, 128), f32)], [VMEM] * 2, 4, 0, 0,
            )(op, src, turn)
    pieces = []
    for p in range(STREAMS // 2):
        ins = []
        for tick in range(top + 1):
            ins += [zs[p][tick - 1]] if tick else []
            for part in (xs, ys) if has_row else (xs,):
                ins += [part[2 * p + slot][tick - 1] for slot in range(2)] if tick else []
            ins += [mids[2 * p + slot][tick] for slot in range(2)] if tick < top else []
        base = 2 * p * width
        mine, other = call(
            functools.partial(last_kernel, top, trace, width, base, has_row),
            [SMEM] * 2 + [VMEM] * (4 + len(ins)), [shaped((rows, 2 * width))] * 2, [VMEM] * 2, 4, 0, 0,
        )(level, parity, both, s, given, turn, *ins)
        back = lax.ppermute(other, "gy", swap)
        turn = mine
        for side, part in enumerate((mine, back)):
            if len(pieces) == STREAMS - 1:
                out = call(
                    functools.partial(final_kernel, half), [SMEM] + [VMEM] * (4 + len(pieces)),
                    shaped((inner, columns)), HBM, 6, 0, 0,
                    scratch=[pltpu.VMEM((inner, columns), bf16), pltpu.SemaphoreType.DMA((BLOCKS,))],
                )(parity, op, r, part, turn, *pieces)
            else:
                piece, turn = call(
                    functools.partial(solve_kernel, half, base, side), [SMEM] + [VMEM] * 4,
                    [shaped((inner, 2 * width)), shaped((8, 128), f32)], [VMEM] * 2, 4, 0, 0,
                )(parity, op, r, part, turn)
                pieces.append(piece)
    return out[None, None, None]


def solution(mesh):
    spec = P("depth", "gx", "gy", None, None)
    sizes = tuple(mesh.shape[a] for a in AXES)
    return jax.shard_map(
        functools.partial(shards, sizes), mesh=mesh, in_specs=(spec, spec), out_specs=spec, check_vma=False
    )
```

profile of v0, /device:TPU:31, one launch (start us, length us, event | category | flops | bytes accessed | tf_op | source)
XLA Modules:
  0.0 122.2 jit_solution(4996029930913094332)
XLA Ops:
  0.0 1.9 %slice.3.op_ref = bf16[768,1536]{1,0:T(8,128)(2,1)S(1)} slice(bf16[1536,1536]{1,0:T(8,128)(2,1)} %bitcast.6), slice={[0:768], [0:1536]} | slice | bytes 4718592 | tf_op jit(solution)/shard_map/slice | solution.py:287
  2.2 0.8 shard_map.29.turn_ref
  3.0 0.7 collective-permute-start.1
  4.2 1.1 shard_map.30.turn_ref.s_ref
  5.4 1.9 %collective-permute-done.mid_ref = bf16[768,256]{1,0:T(8,128)(2,1)S(1)} collective-permute-done((bf16[768,256]{1,0:T(8,128)(2,1)S(1)}, bf16[768,256]{1,0:T(8,128)(2,1)S(1)}, u32[]{:S(2)}, u32[]{:S(2)}) %collective-permute-start) | collective-permute-done | bytes 393248 | tf_op jit(solution)/shard_map/ppermute | solution.py:292
  7.5 0.7 collective-permute-start.8
  8.1 0.7 collective-permute-start.6
  8.8 0.7 collective-permute-start.7
  9.6 0.7 collective-permute-start.5
  10.2 0.7 collective-permute-start.3
  11.2 0.7 collective-permute-start.10
  11.9 0.7 collective-permute-start.4
  12.5 0.7 collective-permute-start.9
  13.2 0.7 collective-permute-start.12
  14.0 0.7 collective-permute-start.17
  14.7 0.7 collective-permute-start.15
  15.4 0.7 collective-permute-start.14
  16.1 0.7 collective-permute-start.16
  16.8 0.7 collective-permute-start.11
  17.5 0.7 collective-permute-start.13
  18.2 0.7 collective-permute-start.18
  18.9 0.7 collective-permute-start.19
  19.7 0.7 collective-permute-start.26
  20.4 0.7 collective-permute-start.21
  21.1 1.3 %collective-permute-start.24 = (bf16[512,128]{1,0:T(8,128)(2,1)S(1)}, bf16[512,128]{1,0:T(8,128)(2,1)S(1)}, u32[]{:S(2)}, u32[]{:S(2)}) collective-permute-start(bf16[512,128]{1,0:T(8,128)(2,1)S(1)} %get-tuple-element.125), channel_id=1, source_target_pairs={{6,8},{7,9},{20,22},{21,23},{28,30},{29,31}} | collective-permute-start | bytes 393224 | tf_op jit(solution)/shard_map/ppermute | solution.py:327
  22.4 1.3 %collective-permute-start.25 = (bf16[512,128]{1,0:T(8,128)(2,1)S(1)}, bf16[512,128]{1,0:T(8,128)(2,1)S(1)}, u32[]{:S(2)}, u32[]{:S(2)}) collective-permute-start(bf16[512,128]{1,0:T(8,128)(2,1)S(1)} %get-tuple-element.126), channel_id=1, source_target_pairs={{6,8},{7,9},{20,22},{21,23},{28,30},{29,31}} | collective-permute-start | bytes 393224 | tf_op jit(solution)/shard_map/ppermute | solution.py:327
  23.7 0.7 collective-permute-start.23
  24.4 17.0 %collective-permute-done.24.refs_0_.refs_18_ = bf16[512,128]{1,0:T(8,128)(2,1)S(1)} collective-permute-done((bf16[512,128]{1,0:T(8,128)(2,1)S(1)}, bf16[512,128]{1,0:T(8,128)(2,1)S(1)}, u32[]{:S(2)}, u32[]{:S(2)}) %collective-permute-start.24) | collective-permute-done | bytes 131104 | tf_op jit(solution)/shard_map/ppermute | solution.py:327
  41.4 1.4 %collective-permute-done.25.refs_0_.refs_1_.refs_19_ = bf16[512,128]{1,0:T(8,128)(2,1)S(1)} collective-permute-done((bf16[512,128]{1,0:T(8,128)(2,1)S(1)}, bf16[512,128]{1,0:T(8,128)(2,1)S(1)}, u32[]{:S(2)}, u32[]{:S(2)}) %collective-permute-start.25) | collective-permute-done | bytes 131104 | tf_op jit(solution)/shard_map/ppermute | solution.py:327
  43.5 1.3 %collective-permute-start.20 = (bf16[512,128]{1,0:T(8,128)(2,1)S(1)}, bf16[512,128]{1,0:T(8,128)(2,1)S(1)}, u32[]{:S(2)}, u32[]{:S(2)}) collective-permute-start(bf16[512,128]{1,0:T(8,128)(2,1)S(1)} %get-tuple-element.120), channel_id=1, source_target_pairs={{6,8},{7,9},{20,22},{21,23},{28,30},{29,31}} | collective-permute-start | bytes 393224 | tf_op jit(solution)/shard_map/ppermute | solution.py:327
  44.8 1.3 %collective-permute-start.22 = (bf16[512,128]{1,0:T(8,128)(2,1)S(1)}, bf16[512,128]{1,0:T(8,128)(2,1)S(1)}, u32[]{:S(2)}, u32[]{:S(2)}) collective-permute-start(bf16[512,128]{1,0:T(8,128)(2,1)S(1)} %get-tuple-element.123), channel_id=1, source_target_pairs={{6,8},{7,9},{20,22},{21,23},{28,30},{29,31}} | collective-permute-start | bytes 393224 | tf_op jit(solution)/shard_map/ppermute | solution.py:327
  46.1 0.7 collective-permute-start.27
  46.8 2.7 %collective-permute-done.20.refs_0_.refs_18_ = bf16[512,128]{1,0:T(8,128)(2,1)S(1)} collective-permute-done((bf16[512,128]{1,0:T(8,128)(2,1)S(1)}, bf16[512,128]{1,0:T(8,128)(2,1)S(1)}, u32[]{:S(2)}, u32[]{:S(2)}) %collective-permute-start.20) | collective-permute-done | bytes 131104 | tf_op jit(solution)/shard_map/ppermute | solution.py:327
  50.2 0.7 collective-permute-done.22.refs_0_.refs_1_.refs_19_
  50.9 1.5 %slice-done = s8[4194304]{0:T(1024)(128)(4,1)S(1)} async-done(((s8[4718592]{0:T(1024)(128)(4,1)}), s8[4194304]{0:T(1024)(128)(4,1)S(1)}, s32[]{:S(2)}) %slice-start) | async-done | bytes 4194328
  52.6 1.7 %shard_map.63 = (f32[768,1024]{1,0:T(8,128)S(1)}, f32[8,128]{1,0:T(8,128)S(1)}) custom-call(bf16[1536,1536]{1,0:T(8,128)(2,1)S(1)} %bitcast.9, bf16[768,1024]{1,0:T(8,128)(2,1)S(1)} %bitcast.17, bf16[1024,128]{1,0:T(8,128)(2,1)S(1)} %shard_map.62.turn_ref), custom_call_target="tpu_custom_call" | custom-call | tf_op jit(solution)/shard_map/pallas_call | solution.py:346
  54.3 0.7 collective-permute-start.35
  55.1 0.7 collective-permute-start.32
  55.8 0.7 collective-permute-start.33
  56.5 0.7 collective-permute-start.34
  57.1 0.7 collective-permute-start.29
  57.8 0.7 collective-permute-start.31
  58.6 0.7 collective-permute-start.37
  59.4 0.7 collective-permute-start.44
  60.0 0.7 collective-permute-start.36
  62.1 0.7 collective-permute-start.43
  62.8 0.7 collective-permute-start.38
  63.5 0.7 collective-permute-start.41
  64.3 1.3 %collective-permute-start.45 = (bf16[1024,128]{1,0:T(8,128)(2,1)S(1)}, bf16[1024,128]{1,0:T(8,128)(2,1)S(1)}, u32[]{:S(2)}, u32[]{:S(2)}) collective-permute-start(bf16[1024,128]{1,0:T(8,128)(2,1)S(1)} %shard_map.78.turn_ref), channel_id=1, source_target_pairs={{14,30},{15,31}} | collective-permute-start | bytes 786440 | tf_op jit(solution)/shard_map/ppermute | solution.py:342
  65.6 0.7 collective-permute-start.40
  66.3 1.3 %collective-permute-start.46 = (bf16[512,128]{1,0:T(8,128)(2,1)S(1)}, bf16[512,128]{1,0:T(8,128)(2,1)S(1)}, u32[]{:S(2)}, u32[]{:S(2)}) collective-permute-start(bf16[512,128]{1,0:T(8,128)(2,1)S(1)} %get-tuple-element.157), channel_id=1, source_target_pairs={{6,8},{7,9},{20,22},{21,23},{28,30},{29,31}} | collective-permute-start | bytes 393224 | tf_op jit(solution)/shard_map/ppermute | solution.py:327
  67.6 1.3 %collective-permute-start.47 = (bf16[512,128]{1,0:T(8,128)(2,1)S(1)}, bf16[512,128]{1,0:T(8,128)(2,1)S(1)}, u32[]{:S(2)}, u32[]{:S(2)}) collective-permute-start(bf16[512,128]{1,0:T(8,128)(2,1)S(1)} %get-tuple-element.158), channel_id=1, source_target_pairs={{6,8},{7,9},{20,22},{21,23},{28,30},{29,31}} | collective-permute-start | bytes 393224 | tf_op jit(solution)/shard_map/ppermute | solution.py:327
  69.0 18.0 %collective-permute-done.46.refs_38_ = bf16[512,128]{1,0:T(8,128)(2,1)S(1)} collective-permute-done((bf16[512,128]{1,0:T(8,128)(2,1)S(1)}, bf16[512,128]{1,0:T(8,128)(2,1)S(1)}, u32[]{:S(2)}, u32[]{:S(2)}) %collective-permute-start.46) | collective-permute-done | bytes 131104 | tf_op jit(solution)/shard_map/ppermute | solution.py:327
  87.0 1.4 %collective-permute-done.47.refs_39_ = bf16[512,128]{1,0:T(8,128)(2,1)S(1)} collective-permute-done((bf16[512,128]{1,0:T(8,128)(2,1)S(1)}, bf16[512,128]{1,0:T(8,128)(2,1)S(1)}, u32[]{:S(2)}, u32[]{:S(2)}) %collective-permute-start.47) | collective-permute-done | bytes 131104 | tf_op jit(solution)/shard_map/ppermute | solution.py:327
  88.4 5.2 %collective-permute-done.45.refs_37_ = bf16[1024,128]{1,0:T(8,128)(2,1)S(1)} collective-permute-done((bf16[1024,128]{1,0:T(8,128)(2,1)S(1)}, bf16[1024,128]{1,0:T(8,128)(2,1)S(1)}, u32[]{:S(2)}, u32[]{:S(2)}) %collective-permute-start.45) | collective-permute-done | bytes 262176 | tf_op jit(solution)/shard_map/ppermute | solution.py:342
  94.0 12.7 %collective-permute-start.48 = (bf16[768,256]{1,0:T(8,128)(2,1)S(1)}, bf16[768,256]{1,0:T(8,128)(2,1)S(1)}, u32[]{:S(2)}, u32[]{:S(2)}) collective-permute-start(bf16[768,256]{1,0:T(8,128)(2,1)S(1)} %get-tuple-element.159), channel_id=1, source_target_pairs={{0,1},{1,0},{2,3},{3,2},{4,5},{5,4},{6,7},{7,6},{8,9},{9,8},{10,11... | collective-permute-start | bytes 1179656 | tf_op jit(solution)/shard_map/ppermute | solution.py:363
  106.7 1.3 %collective-permute-start.49 = (bf16[1024,128]{1,0:T(8,128)(2,1)S(1)}, bf16[1024,128]{1,0:T(8,128)(2,1)S(1)}, u32[]{:S(2)}, u32[]{:S(2)}) collective-permute-start(bf16[1024,128]{1,0:T(8,128)(2,1)S(1)} %shard_map.81.turn_ref), channel_id=1, source_target_pairs={{14,30},{15,31}} | collective-permute-start | bytes 786440 | tf_op jit(solution)/shard_map/ppermute | solution.py:342
  108.0 1.3 %collective-permute-start.50 = (bf16[512,128]{1,0:T(8,128)(2,1)S(1)}, bf16[512,128]{1,0:T(8,128)(2,1)S(1)}, u32[]{:S(2)}, u32[]{:S(2)}) collective-permute-start(bf16[512,128]{1,0:T(8,128)(2,1)S(1)} %get-tuple-element.163), channel_id=1, source_target_pairs={{6,8},{7,9},{20,22},{21,23},{28,30},{29,31}} | collective-permute-start | bytes 393224 | tf_op jit(solution)/shard_map/ppermute | solution.py:327
  109.3 1.3 %collective-permute-start.51 = (bf16[512,128]{1,0:T(8,128)(2,1)S(1)}, bf16[512,128]{1,0:T(8,128)(2,1)S(1)}, u32[]{:S(2)}, u32[]{:S(2)}) collective-permute-start(bf16[512,128]{1,0:T(8,128)(2,1)S(1)} %get-tuple-element.164), channel_id=1, source_target_pairs={{6,8},{7,9},{20,22},{21,23},{28,30},{29,31}} | collective-permute-start | bytes 393224 | tf_op jit(solution)/shard_map/ppermute | solution.py:327
  111.6 3.3 %collective-permute-done.50.refs_38_ = bf16[512,128]{1,0:T(8,128)(2,1)S(1)} collective-permute-done((bf16[512,128]{1,0:T(8,128)(2,1)S(1)}, bf16[512,128]{1,0:T(8,128)(2,1)S(1)}, u32[]{:S(2)}, u32[]{:S(2)}) %collective-permute-start.50) | collective-permute-done | bytes 131104 | tf_op jit(solution)/shard_map/ppermute | solution.py:327
  114.9 2.8 %collective-permute-done.51.refs_39_ = bf16[512,128]{1,0:T(8,128)(2,1)S(1)} collective-permute-done((bf16[512,128]{1,0:T(8,128)(2,1)S(1)}, bf16[512,128]{1,0:T(8,128)(2,1)S(1)}, u32[]{:S(2)}, u32[]{:S(2)}) %collective-permute-start.51) | collective-permute-done | bytes 131104 | tf_op jit(solution)/shard_map/ppermute | solution.py:327
  118.1 0.9 collective-permute-start.52
  119.5 0.9 collective-permute-done.52.in_ref
  120.3 1.7 %shard_map.87 = bf16[768,1024]{1,0:T(8,128)(2,1)} custom-call(s32[1]{0:T(128)} %bitcast.3.parity_ref, bf16[1536,1536]{1,0:T(8,128)(2,1)S(1)} %bitcast.13, f32[768,1024]{1,0:T(8,128)S(1)} %get-tuple-element.131.r_ref, bf16[768,256]{1,0:T(8,128)(2,1)S(1)} %collective-permute-done.52.in_ref, f32[8,128]{1,0:T(8,128)S(1)} %get-tuple-element.167.turn_ref, ...), custom_call_target="tpu_custom_call" | custom-call | tf_op jit(solution)/shard_map/pallas_call | solution.py:367
  (110 shorter events, 6.7 us)
Async XLA Ops:
  0.0 2.1 %copy-start = (bf16[1,1,1,768,1024]{4,3,2,1,0:T(8,128)(2,1)S(1)}, bf16[1,1,1,768,1024]{4,3,2,1,0:T(8,128)(2,1)}, u32[]{:S(2)}) copy-start(bf16[1,1,1,768,1024]{4,3,2,1,0:T(8,128)(2,1)} %param.3) | copy-start | bytes 4718596
  3.0 4.4 %collective-permute-start.1 = (bf16[768,512]{1,0:T(8,128)(2,1)S(1)}, bf16[768,512]{1,0:T(8,128)(2,1)S(1)}, u32[]{:S(2)}, u32[]{:S(2)}) collective-permute-start(bf16[768,512]{1,0:T(8,128)(2,1)S(1)} %shard_map.29.turn_ref), channel_id=1, source_target_pairs={{0,1},{1,0},{2,3},{3,2},{4,5},{5,4},{6,7},{7,6},{8,9},{9,8},{10,11... | collective-permute-start | bytes 2359304 | tf_op jit(solution)/shard_map/ppermute | solution.py:296
  3.7 6.5 %collective-permute-start.2 = (bf16[768,512]{1,0:T(8,128)(2,1)S(1)}, bf16[768,512]{1,0:T(8,128)(2,1)S(1)}, u32[]{:S(2)}, u32[]{:S(2)}) collective-permute-start(bf16[768,512]{1,0:T(8,128)(2,1)S(1)} %get-tuple-element.98), channel_id=1, source_target_pairs={{0,1},{1,0},{2,3},{3,2},{4,5},{5,4},{6,7},{7,6},{8,9},{9,8},{10,11... | collective-permute-start | bytes 2359304 | tf_op jit(solution)/shard_map/ppermute | solution.py:297
  3.8 3.5 %collective-permute-start = (bf16[768,256]{1,0:T(8,128)(2,1)S(1)}, bf16[768,256]{1,0:T(8,128)(2,1)S(1)}, u32[]{:S(2)}, u32[]{:S(2)}) collective-permute-start(bf16[768,256]{1,0:T(8,128)(2,1)S(1)} %get-tuple-element.93.turn_ref), channel_id=1, source_target_pairs={{0,1},{1,0},{2,3},{3,2},{4,5},{5,4},{6,7},{7,6},{8,9},{9,8},{10,11... | collective-permute-start | bytes 1179656 | tf_op jit(solution)/shard_map/ppermute | solution.py:292
  7.5 3.6 %collective-permute-start.8 = (bf16[1024,128]{1,0:T(8,128)(2,1)S(1)}, bf16[1024,128]{1,0:T(8,128)(2,1)S(1)}, u32[]{:S(2)}, u32[]{:S(2)}) collective-permute-start(bf16[1024,128]{1,0:T(8,128)(2,1)S(1)} %shard_map.34.turn_ref), channel_id=1, source_target_pairs={{0,16},{1,17}} | collective-permute-start | bytes 786440 | tf_op jit(solution)/shard_map/ppermute | solution.py:342
  8.1 3.0 %collective-permute-start.6 = (bf16[512,128]{1,0:T(8,128)(2,1)S(1)}, bf16[512,128]{1,0:T(8,128)(2,1)S(1)}, u32[]{:S(2)}, u32[]{:S(2)}) collective-permute-start(bf16[512,128]{1,0:T(8,128)(2,1)S(1)} %get-tuple-element.101), channel_id=1, source_target_pairs={{0,2},{1,3},{8,10},{9,11},{22,24},{23,25}} | collective-permute-start | bytes 393224 | tf_op jit(solution)/shard_map/ppermute | solution.py:327
  8.8 2.3 %collective-permute-start.7 = (bf16[512,128]{1,0:T(8,128)(2,1)S(1)}, bf16[512,128]{1,0:T(8,128)(2,1)S(1)}, u32[]{:S(2)}, u32[]{:S(2)}) collective-permute-start(bf16[512,128]{1,0:T(8,128)(2,1)S(1)} %get-tuple-element.102), channel_id=1, source_target_pairs={{0,2},{1,3},{8,10},{9,11},{22,24},{23,25}} | collective-permute-start | bytes 393224 | tf_op jit(solution)/shard_map/ppermute | solution.py:327
  9.6 4.4 %collective-permute-start.5 = (bf16[1024,128]{1,0:T(8,128)(2,1)S(1)}, bf16[1024,128]{1,0:T(8,128)(2,1)S(1)}, u32[]{:S(2)}, u32[]{:S(2)}) collective-permute-start(bf16[1024,128]{1,0:T(8,128)(2,1)S(1)} %shard_map.37.turn_ref), channel_id=1, source_target_pairs={{0,16},{1,17}} | collective-permute-start | bytes 786440 | tf_op jit(solution)/shard_map/ppermute | solution.py:342
  10.2 3.0 %collective-permute-start.3 = (bf16[512,128]{1,0:T(8,128)(2,1)S(1)}, bf16[512,128]{1,0:T(8,128)(2,1)S(1)}, u32[]{:S(2)}, u32[]{:S(2)}) collective-permute-start(bf16[512,128]{1,0:T(8,128)(2,1)S(1)} %get-tuple-element.99), channel_id=1, source_target_pairs={{0,2},{1,3},{8,10},{9,11},{22,24},{23,25}} | collective-permute-start | bytes 393224 | tf_op jit(solution)/shard_map/ppermute | solution.py:327
  11.2 4.2 %collective-permute-start.10 = (bf16[1024,128]{1,0:T(8,128)(2,1)S(1)}, bf16[1024,128]{1,0:T(8,128)(2,1)S(1)}, u32[]{:S(2)}, u32[]{:S(2)}) collective-permute-start(bf16[1024,128]{1,0:T(8,128)(2,1)S(1)} %shard_map.41.turn_ref), channel_id=1, source_target_pairs={{2,18},{3,19}} | collective-permute-start | bytes 786440 | tf_op jit(solution)/shard_map/ppermute | solution.py:342
  11.9 2.1 %collective-permute-start.4 = (bf16[512,128]{1,0:T(8,128)(2,1)S(1)}, bf16[512,128]{1,0:T(8,128)(2,1)S(1)}, u32[]{:S(2)}, u32[]{:S(2)}) collective-permute-start(bf16[512,128]{1,0:T(8,128)(2,1)S(1)} %get-tuple-element.100), channel_id=1, source_target_pairs={{0,2},{1,3},{8,10},{9,11},{22,24},{23,25}} | collective-permute-start | bytes 393224 | tf_op jit(solution)/shard_map/ppermute | solution.py:327
  12.5 2.8 %collective-permute-start.9 = (bf16[512,128]{1,0:T(8,128)(2,1)S(1)}, bf16[512,128]{1,0:T(8,128)(2,1)S(1)}, u32[]{:S(2)}, u32[]{:S(2)}) collective-permute-start(bf16[512,128]{1,0:T(8,128)(2,1)S(1)} %get-tuple-element.107), channel_id=1, source_target_pairs={{2,4},{3,5},{10,12},{11,13},{16,18},{17,19},{24,26},{25,27}} | collective-permute-start | bytes 393224 | tf_op jit(solution)/shard_map/ppermute | solution.py:327
  13.2 2.2 %collective-permute-start.12 = (bf16[512,128]{1,0:T(8,128)(2,1)S(1)}, bf16[512,128]{1,0:T(8,128)(2,1)S(1)}, u32[]{:S(2)}, u32[]{:S(2)}) collective-permute-start(bf16[512,128]{1,0:T(8,128)(2,1)S(1)} %get-tuple-element.110), channel_id=1, source_target_pairs={{2,4},{3,5},{10,12},{11,13},{16,18},{17,19},{24,26},{25,27}} | collective-permute-start | bytes 393224 | tf_op jit(solution)/shard_map/ppermute | solution.py:327
  14.0 4.2 %collective-permute-start.17 = (bf16[1024,128]{1,0:T(8,128)(2,1)S(1)}, bf16[1024,128]{1,0:T(8,128)(2,1)S(1)}, u32[]{:S(2)}, u32[]{:S(2)}) collective-permute-start(bf16[1024,128]{1,0:T(8,128)(2,1)S(1)} %shard_map.44.turn_ref), channel_id=1, source_target_pairs={{2,18},{3,19}} | collective-permute-start | bytes 786440 | tf_op jit(solution)/shard_map/ppermute | solution.py:342
  14.7 2.8 %collective-permute-start.15 = (bf16[512,128]{1,0:T(8,128)(2,1)S(1)}, bf16[512,128]{1,0:T(8,128)(2,1)S(1)}, u32[]{:S(2)}, u32[]{:S(2)}) collective-permute-start(bf16[512,128]{1,0:T(8,128)(2,1)S(1)} %get-tuple-element.113), channel_id=1, source_target_pairs={{2,4},{3,5},{10,12},{11,13},{16,18},{17,19},{24,26},{25,27}} | collective-permute-start | bytes 393224 | tf_op jit(solution)/shard_map/ppermute | solution.py:327
  15.4 4.2 %collective-permute-start.14 = (bf16[1024,128]{1,0:T(8,128)(2,1)S(1)}, bf16[1024,128]{1,0:T(8,128)(2,1)S(1)}, u32[]{:S(2)}, u32[]{:S(2)}) collective-permute-start(bf16[1024,128]{1,0:T(8,128)(2,1)S(1)} %shard_map.47.turn_ref), channel_id=1, source_target_pairs={{4,20},{5,21}} | collective-permute-start | bytes 786440 | tf_op jit(solution)/shard_map/ppermute | solution.py:342
  16.1 2.8 %collective-permute-start.16 = (bf16[512,128]{1,0:T(8,128)(2,1)S(1)}, bf16[512,128]{1,0:T(8,128)(2,1)S(1)}, u32[]{:S(2)}, u32[]{:S(2)}) collective-permute-start(bf16[512,128]{1,0:T(8,128)(2,1)S(1)} %get-tuple-element.114), channel_id=1, source_target_pairs={{2,4},{3,5},{10,12},{11,13},{16,18},{17,19},{24,26},{25,27}} | collective-permute-start | bytes 393224 | tf_op jit(solution)/shard_map/ppermute | solution.py:327
  16.8 2.8 %collective-permute-start.11 = (bf16[512,128]{1,0:T(8,128)(2,1)S(1)}, bf16[512,128]{1,0:T(8,128)(2,1)S(1)}, u32[]{:S(2)}, u32[]{:S(2)}) collective-permute-start(bf16[512,128]{1,0:T(8,128)(2,1)S(1)} %get-tuple-element.108), channel_id=1, source_target_pairs={{4,6},{5,7},{12,14},{13,15},{18,20},{19,21},{26,28},{27,29}} | collective-permute-start | bytes 393224 | tf_op jit(solution)/shard_map/ppermute | solution.py:327
  17.5 2.2 %collective-permute-start.13 = (bf16[512,128]{1,0:T(8,128)(2,1)S(1)}, bf16[512,128]{1,0:T(8,128)(2,1)S(1)}, u32[]{:S(2)}, u32[]{:S(2)}) collective-permute-start(bf16[512,128]{1,0:T(8,128)(2,1)S(1)} %get-tuple-element.111), channel_id=1, source_target_pairs={{4,6},{5,7},{12,14},{13,15},{18,20},{19,21},{26,28},{27,29}} | collective-permute-start | bytes 393224 | tf_op jit(solution)/shard_map/ppermute | solution.py:327
  18.2 4.2 %collective-permute-start.18 = (bf16[512,128]{1,0:T(8,128)(2,1)S(1)}, bf16[512,128]{1,0:T(8,128)(2,1)S(1)}, u32[]{:S(2)}, u32[]{:S(2)}) collective-permute-start(bf16[512,128]{1,0:T(8,128)(2,1)S(1)} %get-tuple-element.119), channel_id=1, source_target_pairs={{4,6},{5,7},{12,14},{13,15},{18,20},{19,21},{26,28},{27,29}} | collective-permute-start | bytes 393224 | tf_op jit(solution)/shard_map/ppermute | solution.py:327
  18.9 4.8 %collective-permute-start.19 = (bf16[1024,128]{1,0:T(8,128)(2,1)S(1)}, bf16[1024,128]{1,0:T(8,128)(2,1)S(1)}, u32[]{:S(2)}, u32[]{:S(2)}) collective-permute-start(bf16[1024,128]{1,0:T(8,128)(2,1)S(1)} %shard_map.50.turn_ref), channel_id=1, source_target_pairs={{4,20},{5,21}} | collective-permute-start | bytes 786440 | tf_op jit(solution)/shard_map/ppermute | solution.py:342
  19.7 21.7 %collective-permute-start.26 = (bf16[1024,128]{1,0:T(8,128)(2,1)S(1)}, bf16[1024,128]{1,0:T(8,128)(2,1)S(1)}, u32[]{:S(2)}, u32[]{:S(2)}) collective-permute-start(bf16[1024,128]{1,0:T(8,128)(2,1)S(1)} %shard_map.53.turn_ref), channel_id=1, source_target_pairs={{6,22},{7,23}} | collective-permute-start | bytes 786440 | tf_op jit(solution)/shard_map/ppermute | solution.py:342
  20.4 3.3 %collective-permute-start.21 = (bf16[512,128]{1,0:T(8,128)(2,1)S(1)}, bf16[512,128]{1,0:T(8,128)(2,1)S(1)}, u32[]{:S(2)}, u32[]{:S(2)}) collective-permute-start(bf16[512,128]{1,0:T(8,128)(2,1)S(1)} %get-tuple-element.122), channel_id=1, source_target_pairs={{4,6},{5,7},{12,14},{13,15},{18,20},{19,21},{26,28},{27,29}} | collective-permute-start | bytes 393224 | tf_op jit(solution)/shard_map/ppermute | solution.py:327
  21.1 20.4 %collective-permute-start.24 = (bf16[512,128]{1,0:T(8,128)(2,1)S(1)}, bf16[512,128]{1,0:T(8,128)(2,1)S(1)}, u32[]{:S(2)}, u32[]{:S(2)}) collective-permute-start(bf16[512,128]{1,0:T(8,128)(2,1)S(1)} %get-tuple-element.125), channel_id=1, source_target_pairs={{6,8},{7,9},{20,22},{21,23},{28,30},{29,31}} | collective-permute-start | bytes 393224 | tf_op jit(solution)/shard_map/ppermute | solution.py:327
  22.4 20.5 %collective-permute-start.25 = (bf16[512,128]{1,0:T(8,128)(2,1)S(1)}, bf16[512,128]{1,0:T(8,128)(2,1)S(1)}, u32[]{:S(2)}, u32[]{:S(2)}) collective-permute-start(bf16[512,128]{1,0:T(8,128)(2,1)S(1)} %get-tuple-element.126), channel_id=1, source_target_pairs={{6,8},{7,9},{20,22},{21,23},{28,30},{29,31}} | collective-permute-start | bytes 393224 | tf_op jit(solution)/shard_map/ppermute | solution.py:327
  23.7 26.4 %collective-permute-start.23 = (bf16[1024,128]{1,0:T(8,128)(2,1)S(1)}, bf16[1024,128]{1,0:T(8,128)(2,1)S(1)}, u32[]{:S(2)}, u32[]{:S(2)}) collective-permute-start(bf16[1024,128]{1,0:T(8,128)(2,1)S(1)} %shard_map.56.turn_ref), channel_id=1, source_target_pairs={{6,22},{7,23}} | collective-permute-start | bytes 786440 | tf_op jit(solution)/shard_map/ppermute | solution.py:342
  42.8 12.2 %collective-permute-start.28 = (bf16[1024,128]{1,0:T(8,128)(2,1)S(1)}, bf16[1024,128]{1,0:T(8,128)(2,1)S(1)}, u32[]{:S(2)}, u32[]{:S(2)}) collective-permute-start(bf16[1024,128]{1,0:T(8,128)(2,1)S(1)} %shard_map.59.turn_ref), channel_id=1, source_target_pairs={{8,24},{9,25}} | collective-permute-start | bytes 786440 | tf_op jit(solution)/shard_map/ppermute | solution.py:342
  43.5 5.9 %collective-permute-start.20 = (bf16[512,128]{1,0:T(8,128)(2,1)S(1)}, bf16[512,128]{1,0:T(8,128)(2,1)S(1)}, u32[]{:S(2)}, u32[]{:S(2)}) collective-permute-start(bf16[512,128]{1,0:T(8,128)(2,1)S(1)} %get-tuple-element.120), channel_id=1, source_target_pairs={{6,8},{7,9},{20,22},{21,23},{28,30},{29,31}} | collective-permute-start | bytes 393224 | tf_op jit(solution)/shard_map/ppermute | solution.py:327
  44.8 6.0 %collective-permute-start.22 = (bf16[512,128]{1,0:T(8,128)(2,1)S(1)}, bf16[512,128]{1,0:T(8,128)(2,1)S(1)}, u32[]{:S(2)}, u32[]{:S(2)}) collective-permute-start(bf16[512,128]{1,0:T(8,128)(2,1)S(1)} %get-tuple-element.123), channel_id=1, source_target_pairs={{6,8},{7,9},{20,22},{21,23},{28,30},{29,31}} | collective-permute-start | bytes 393224 | tf_op jit(solution)/shard_map/ppermute | solution.py:327
  46.1 8.9 %collective-permute-start.27 = (bf16[512,128]{1,0:T(8,128)(2,1)S(1)}, bf16[512,128]{1,0:T(8,128)(2,1)S(1)}, u32[]{:S(2)}, u32[]{:S(2)}) collective-permute-start(bf16[512,128]{1,0:T(8,128)(2,1)S(1)} %get-tuple-element.133), channel_id=1, source_target_pairs={{0,2},{1,3},{8,10},{9,11},{22,24},{23,25}} | collective-permute-start | bytes 393224 | tf_op jit(solution)/shard_map/ppermute | solution.py:327
  49.5 5.6 %collective-permute-start.30 = (bf16[512,128]{1,0:T(8,128)(2,1)S(1)}, bf16[512,128]{1,0:T(8,128)(2,1)S(1)}, u32[]{:S(2)}, u32[]{:S(2)}) collective-permute-start(bf16[512,128]{1,0:T(8,128)(2,1)S(1)} %get-tuple-element.136), channel_id=1, source_target_pairs={{0,2},{1,3},{8,10},{9,11},{22,24},{23,25}} | collective-permute-start | bytes 393224 | tf_op jit(solution)/shard_map/ppermute | solution.py:327
  50.1 2.2 %slice-start = ((s8[4718592]{0:T(1024)(128)(4,1)}), s8[4194304]{0:T(1024)(128)(4,1)S(1)}, s32[]{:S(2)}) async-start(s8[4718592]{0:T(1024)(128)(4,1)} %bitcast.7), calls=%async_computation | async-start | bytes 8388608
  50.9 1.7 %slice-start.1 = ((s8[4718592]{0:T(1024)(128)(4,1)}), s8[524288]{0:T(1024)(128)(4,1)S(1)}, s32[]{:S(2)}) async-start(s8[4718592]{0:T(1024)(128)(4,1)} %bitcast.7), calls=%async_computation.1 | async-start | bytes 1048576
  54.3 4.2 %collective-permute-start.35 = (bf16[1024,128]{1,0:T(8,128)(2,1)S(1)}, bf16[1024,128]{1,0:T(8,128)(2,1)S(1)}, u32[]{:S(2)}, u32[]{:S(2)}) collective-permute-start(bf16[1024,128]{1,0:T(8,128)(2,1)S(1)} %shard_map.62.turn_ref), channel_id=1, source_target_pairs={{8,24},{9,25}} | collective-permute-start | bytes 786440 | tf_op jit(solution)/shard_map/ppermute | solution.py:342
  55.1 4.2 %collective-permute-start.32 = (bf16[1024,128]{1,0:T(8,128)(2,1)S(1)}, bf16[1024,128]{1,0:T(8,128)(2,1)S(1)}, u32[]{:S(2)}, u32[]{:S(2)}) collective-permute-start(bf16[1024,128]{1,0:T(8,128)(2,1)S(1)} %shard_map.66.turn_ref), channel_id=1, source_target_pairs={{10,26},{11,27}} | collective-permute-start | bytes 786440 | tf_op jit(solution)/shard_map/ppermute | solution.py:342
  55.8 2.0 %collective-permute-start.33 = (bf16[512,128]{1,0:T(8,128)(2,1)S(1)}, bf16[512,128]{1,0:T(8,128)(2,1)S(1)}, u32[]{:S(2)}, u32[]{:S(2)}) collective-permute-start(bf16[512,128]{1,0:T(8,128)(2,1)S(1)} %get-tuple-element.139), channel_id=1, source_target_pairs={{0,2},{1,3},{8,10},{9,11},{22,24},{23,25}} | collective-permute-start | bytes 393224 | tf_op jit(solution)/shard_map/ppermute | solution.py:327
  56.5 2.1 %collective-permute-start.34 = (bf16[512,128]{1,0:T(8,128)(2,1)S(1)}, bf16[512,128]{1,0:T(8,128)(2,1)S(1)}, u32[]{:S(2)}, u32[]{:S(2)}) collective-permute-start(bf16[512,128]{1,0:T(8,128)(2,1)S(1)} %get-tuple-element.140), channel_id=1, source_target_pairs={{0,2},{1,3},{8,10},{9,11},{22,24},{23,25}} | collective-permute-start | bytes 393224 | tf_op jit(solution)/shard_map/ppermute | solution.py:327
  57.1 2.1 %collective-permute-start.29 = (bf16[512,128]{1,0:T(8,128)(2,1)S(1)}, bf16[512,128]{1,0:T(8,128)(2,1)S(1)}, u32[]{:S(2)}, u32[]{:S(2)}) collective-permute-start(bf16[512,128]{1,0:T(8,128)(2,1)S(1)} %get-tuple-element.134), channel_id=1, source_target_pairs={{2,4},{3,5},{10,12},{11,13},{16,18},{17,19},{24,26},{25,27}} | collective-permute-start | bytes 393224 | tf_op jit(solution)/shard_map/ppermute | solution.py:327
  57.8 1.5 %collective-permute-start.31 = (bf16[512,128]{1,0:T(8,128)(2,1)S(1)}, bf16[512,128]{1,0:T(8,128)(2,1)S(1)}, u32[]{:S(2)}, u32[]{:S(2)}) collective-permute-start(bf16[512,128]{1,0:T(8,128)(2,1)S(1)} %get-tuple-element.137), channel_id=1, source_target_pairs={{2,4},{3,5},{10,12},{11,13},{16,18},{17,19},{24,26},{25,27}} | collective-permute-start | bytes 393224 | tf_op jit(solution)/shard_map/ppermute | solution.py:327
  58.6 4.2 %collective-permute-start.37 = (bf16[1024,128]{1,0:T(8,128)(2,1)S(1)}, bf16[1024,128]{1,0:T(8,128)(2,1)S(1)}, u32[]{:S(2)}, u32[]{:S(2)}) collective-permute-start(bf16[1024,128]{1,0:T(8,128)(2,1)S(1)} %shard_map.69.turn_ref), channel_id=1, source_target_pairs={{10,26},{11,27}} | collective-permute-start | bytes 786440 | tf_op jit(solution)/shard_map/ppermute | solution.py:342
  59.4 4.9 %collective-permute-start.44 = (bf16[1024,128]{1,0:T(8,128)(2,1)S(1)}, bf16[1024,128]{1,0:T(8,128)(2,1)S(1)}, u32[]{:S(2)}, u32[]{:S(2)}) collective-permute-start(bf16[1024,128]{1,0:T(8,128)(2,1)S(1)} %shard_map.72.turn_ref), channel_id=1, source_target_pairs={{12,28},{13,29}} | collective-permute-start | bytes 786440 | tf_op jit(solution)/shard_map/ppermute | solution.py:342
  60.0 2.0 %collective-permute-start.36 = (bf16[512,128]{1,0:T(8,128)(2,1)S(1)}, bf16[512,128]{1,0:T(8,128)(2,1)S(1)}, u32[]{:S(2)}, u32[]{:S(2)}) collective-permute-start(bf16[512,128]{1,0:T(8,128)(2,1)S(1)} %get-tuple-element.145), channel_id=1, source_target_pairs={{2,4},{3,5},{10,12},{11,13},{16,18},{17,19},{24,26},{25,27}} | collective-permute-start | bytes 393224 | tf_op jit(solution)/shard_map/ppermute | solution.py:327
  60.7 2.8 %collective-permute-start.39 = (bf16[512,128]{1,0:T(8,128)(2,1)S(1)}, bf16[512,128]{1,0:T(8,128)(2,1)S(1)}, u32[]{:S(2)}, u32[]{:S(2)}) collective-permute-start(bf16[512,128]{1,0:T(8,128)(2,1)S(1)} %get-tuple-element.148), channel_id=1, source_target_pairs={{2,4},{3,5},{10,12},{11,13},{16,18},{17,19},{24,26},{25,27}} | collective-permute-start | bytes 393224 | tf_op jit(solution)/shard_map/ppermute | solution.py:327
  61.4 2.8 %collective-permute-start.42 = (bf16[512,128]{1,0:T(8,128)(2,1)S(1)}, bf16[512,128]{1,0:T(8,128)(2,1)S(1)}, u32[]{:S(2)}, u32[]{:S(2)}) collective-permute-start(bf16[512,128]{1,0:T(8,128)(2,1)S(1)} %get-tuple-element.151), channel_id=1, source_target_pairs={{4,6},{5,7},{12,14},{13,15},{18,20},{19,21},{26,28},{27,29}} | collective-permute-start | bytes 393224 | tf_op jit(solution)/shard_map/ppermute | solution.py:327
  62.1 2.2 %collective-permute-start.43 = (bf16[512,128]{1,0:T(8,128)(2,1)S(1)}, bf16[512,128]{1,0:T(8,128)(2,1)S(1)}, u32[]{:S(2)}, u32[]{:S(2)}) collective-permute-start(bf16[512,128]{1,0:T(8,128)(2,1)S(1)} %get-tuple-element.152), channel_id=1, source_target_pairs={{4,6},{5,7},{12,14},{13,15},{18,20},{19,21},{26,28},{27,29}} | collective-permute-start | bytes 393224 | tf_op jit(solution)/shard_map/ppermute | solution.py:327
  62.8 4.8 %collective-permute-start.38 = (bf16[512,128]{1,0:T(8,128)(2,1)S(1)}, bf16[512,128]{1,0:T(8,128)(2,1)S(1)}, u32[]{:S(2)}, u32[]{:S(2)}) collective-permute-start(bf16[512,128]{1,0:T(8,128)(2,1)S(1)} %get-tuple-element.146), channel_id=1, source_target_pairs={{4,6},{5,7},{12,14},{13,15},{18,20},{19,21},{26,28},{27,29}} | collective-permute-start | bytes 393224 | tf_op jit(solution)/shard_map/ppermute | solution.py:327
  63.5 5.4 %collective-permute-start.41 = (bf16[1024,128]{1,0:T(8,128)(2,1)S(1)}, bf16[1024,128]{1,0:T(8,128)(2,1)S(1)}, u32[]{:S(2)}, u32[]{:S(2)}) collective-permute-start(bf16[1024,128]{1,0:T(8,128)(2,1)S(1)} %shard_map.75.turn_ref), channel_id=1, source_target_pairs={{12,28},{13,29}} | collective-permute-start | bytes 786440 | tf_op jit(solution)/shard_map/ppermute | solution.py:342
  64.3 29.3 %collective-permute-start.45 = (bf16[1024,128]{1,0:T(8,128)(2,1)S(1)}, bf16[1024,128]{1,0:T(8,128)(2,1)S(1)}, u32[]{:S(2)}, u32[]{:S(2)}) collective-permute-start(bf16[1024,128]{1,0:T(8,128)(2,1)S(1)} %shard_map.78.turn_ref), channel_id=1, source_target_pairs={{14,30},{15,31}} | collective-permute-start | bytes 786440 | tf_op jit(solution)/shard_map/ppermute | solution.py:342
  65.6 3.3 %collective-permute-start.40 = (bf16[512,128]{1,0:T(8,128)(2,1)S(1)}, bf16[512,128]{1,0:T(8,128)(2,1)S(1)}, u32[]{:S(2)}, u32[]{:S(2)}) collective-permute-start(bf16[512,128]{1,0:T(8,128)(2,1)S(1)} %get-tuple-element.149), channel_id=1, source_target_pairs={{4,6},{5,7},{12,14},{13,15},{18,20},{19,21},{26,28},{27,29}} | collective-permute-start | bytes 393224 | tf_op jit(solution)/shard_map/ppermute | solution.py:327
  66.3 20.7 %collective-permute-start.46 = (bf16[512,128]{1,0:T(8,128)(2,1)S(1)}, bf16[512,128]{1,0:T(8,128)(2,1)S(1)}, u32[]{:S(2)}, u32[]{:S(2)}) collective-permute-start(bf16[512,128]{1,0:T(8,128)(2,1)S(1)} %get-tuple-element.157), channel_id=1, source_target_pairs={{6,8},{7,9},{20,22},{21,23},{28,30},{29,31}} | collective-permute-start | bytes 393224 | tf_op jit(solution)/shard_map/ppermute | solution.py:327
  67.6 20.8 %collective-permute-start.47 = (bf16[512,128]{1,0:T(8,128)(2,1)S(1)}, bf16[512,128]{1,0:T(8,128)(2,1)S(1)}, u32[]{:S(2)}, u32[]{:S(2)}) collective-permute-start(bf16[512,128]{1,0:T(8,128)(2,1)S(1)} %get-tuple-element.158), channel_id=1, source_target_pairs={{6,8},{7,9},{20,22},{21,23},{28,30},{29,31}} | collective-permute-start | bytes 393224 | tf_op jit(solution)/shard_map/ppermute | solution.py:327
  94.0 17.1 %collective-permute-start.48 = (bf16[768,256]{1,0:T(8,128)(2,1)S(1)}, bf16[768,256]{1,0:T(8,128)(2,1)S(1)}, u32[]{:S(2)}, u32[]{:S(2)}) collective-permute-start(bf16[768,256]{1,0:T(8,128)(2,1)S(1)} %get-tuple-element.159), channel_id=1, source_target_pairs={{0,1},{1,0},{2,3},{3,2},{4,5},{5,4},{6,7},{7,6},{8,9},{9,8},{10,11... | collective-permute-start | bytes 1179656 | tf_op jit(solution)/shard_map/ppermute | solution.py:363
  106.7 11.1 %collective-permute-start.49 = (bf16[1024,128]{1,0:T(8,128)(2,1)S(1)}, bf16[1024,128]{1,0:T(8,128)(2,1)S(1)}, u32[]{:S(2)}, u32[]{:S(2)}) collective-permute-start(bf16[1024,128]{1,0:T(8,128)(2,1)S(1)} %shard_map.81.turn_ref), channel_id=1, source_target_pairs={{14,30},{15,31}} | collective-permute-start | bytes 786440 | tf_op jit(solution)/shard_map/ppermute | solution.py:342
  108.0 6.9 %collective-permute-start.50 = (bf16[512,128]{1,0:T(8,128)(2,1)S(1)}, bf16[512,128]{1,0:T(8,128)(2,1)S(1)}, u32[]{:S(2)}, u32[]{:S(2)}) collective-permute-start(bf16[512,128]{1,0:T(8,128)(2,1)S(1)} %get-tuple-element.163), channel_id=1, source_target_pairs={{6,8},{7,9},{20,22},{21,23},{28,30},{29,31}} | collective-permute-start | bytes 393224 | tf_op jit(solution)/shard_map/ppermute | solution.py:327
  109.3 8.4 %collective-permute-start.51 = (bf16[512,128]{1,0:T(8,128)(2,1)S(1)}, bf16[512,128]{1,0:T(8,128)(2,1)S(1)}, u32[]{:S(2)}, u32[]{:S(2)}) collective-permute-start(bf16[512,128]{1,0:T(8,128)(2,1)S(1)} %get-tuple-element.164), channel_id=1, source_target_pairs={{6,8},{7,9},{20,22},{21,23},{28,30},{29,31}} | collective-permute-start | bytes 393224 | tf_op jit(solution)/shard_map/ppermute | solution.py:327
  118.1 2.2 %collective-permute-start.52 = (bf16[768,256]{1,0:T(8,128)(2,1)S(1)}, bf16[768,256]{1,0:T(8,128)(2,1)S(1)}, u32[]{:S(2)}, u32[]{:S(2)}) collective-permute-start(bf16[768,256]{1,0:T(8,128)(2,1)S(1)} %get-tuple-element.165), channel_id=1, source_target_pairs={{0,1},{1,0},{2,3},{3,2},{4,5},{5,4},{6,7},{7,6},{8,9},{9,8},{10,11... | collective-permute-start | bytes 1179656 | tf_op jit(solution)/shard_map/ppermute | solution.py:363
where the time goes:
time: 123 us; the launch traced here: 122 us
  waiting for transfers between devices  55.6 us (45%)
  starting transfers between devices  53.2 us (43%)
  Pallas kernels  8.24 us (7%)
  local copies, waits for them, and re-layouts  3.86 us (3%)
  between operations  1.29 us (1%)
    ppermute x32, waiting for transfers between devices, shards(): xs[n].append(lax.ppermute(sent[0], AXES, route(sizes, 1, tick)))  47.4 us
    ppermute x32, starting transfers between devices, shards(): xs[n].append(lax.ppermute(sent[0], AXES, route(sizes, 1, tick)))  26.4 us
    ppermute x2, starting transfers between devices, shards(): back = lax.ppermute(other, 'gy', swap)  13.6 us
    ppermute x16, starting transfers between devices, shards(): zs[n // 2].append(lax.ppermute(turn, AXES, route(sizes, 0, tick)))  12 us
    ppermute x16, waiting for transfers between devices, shards(): zs[n // 2].append(lax.ppermute(turn, AXES, route(sizes, 0, tick)))  5.38 us
  transfers between devices with their start and end apart: 53, of which 12 were waited for; matrix products, arithmetic and copies ran while one was open for 0% of the time, Pallas kernels for 4%

commit v1 on v0

--- a/solution.py
+++ b/solution.py
@@ -8,7 +8,7 @@
 
 STREAMS = 4
 BLOCKS = 2
-REPEAT = (8, 4, 4)
+REPEAT = (8, (5, 4, 4, 4), 4)
 VMEM = pl.BlockSpec(memory_space=pltpu.VMEM)
 SMEM = pl.BlockSpec(memory_space=pltpu.SMEM)
 HBM = pl.BlockSpec(memory_space=pltpu.HBM)
@@ -38,7 +38,7 @@
     )
 
 
-def route(sizes, axis, tick):
+def route(sizes, axis, tick, repeat):
     nd, nx, ny = sizes
     pairs = []
     for d in range(nd):
@@ -47,7 +47,7 @@
                 group = j // 2
                 at, to = [d, i, group], [d, i, group]
                 to[axis] += 1
-                if to[axis] < (nd, nx, ny // 2)[axis] and (sum(at) - tick) % REPEAT[axis] == 0:
+                if to[axis] < (nd, nx, ny // 2)[axis] and (sum(at) - tick) % repeat == 0:
                     end = (to[0] * nx + to[1]) * ny + 2 * to[2] + j % 2
                     pairs.append(((d * nx + i) * ny + j, end))
     return pairs
@@ -324,9 +324,9 @@
             )(level, parity, both, s, given, *ins)
             turn = sent[1]
             mids[n].append(turn)
-            xs[n].append(lax.ppermute(sent[0], AXES, route(sizes, 1, tick)))
+            xs[n].append(lax.ppermute(sent[0], AXES, route(sizes, 1, tick, REPEAT[1][n])))
             if has_row:
-                ys[n].append(lax.ppermute(sent[2], AXES, route(sizes, 2, tick)))
+                ys[n].append(lax.ppermute(sent[2], AXES, route(sizes, 2, tick, REPEAT[2])))
             if slot:
                 both_slots = (n - 1, n)
                 ins = []
@@ -339,7 +339,7 @@
                     functools.partial(depth_kernel, tick, trace, cols, tick > 0, has_row),
                     [SMEM] * 3 + [VMEM] * (3 + len(ins)), shaped((4 * trace, width)), VMEM, 4, 0, 0,
                 )(level, parity, more, both, s, given, *ins)
-                zs[n // 2].append(lax.ppermute(turn, AXES, route(sizes, 0, tick)))
+                zs[n // 2].append(lax.ppermute(turn, AXES, route(sizes, 0, tick, REPEAT[0])))
         if tick == 0:
             both = turn = joined(turn, rest_got)
         if tick == top // 2:

time: 123 us -> 123 us (level)
  no operation moved by 1% of the time
where the time goes in v1:
time: 123 us; the launch traced here: 122 us
  waiting for transfers between devices  55.6 us (45%)
  starting transfers between devices  53.2 us (43%)
  Pallas kernels  8.24 us (7%)
  local copies, waits for them, and re-layouts  3.86 us (3%)
  between operations  1.28 us (1%)
    ppermute x32, waiting for transfers between devices, shards(): lax.ppermute(sent[0], AXES, route(sizes, 1, tick, REPEAT[1][n]))  47.4 us
    ppermute x32, starting transfers between devices, shards(): lax.ppermute(sent[0], AXES, route(sizes, 1, tick, REPEAT[1][n]))  26.4 us
    ppermute x2, starting transfers between devices, shards(): back = lax.ppermute(other, 'gy', swap)  13.6 us
    ppermute x16, starting transfers between devices, shards(): lax.ppermute(turn, AXES, route(sizes, 0, tick, REPEAT[0]))  12 us
    ppermute x16, waiting for transfers between devices, shards(): lax.ppermute(turn, AXES, route(sizes, 0, tick, REPEAT[0]))  5.38 us
  transfers between devices with their start and end apart: 53, of which 12 were waited for; matrix products, arithmetic and copies ran while one was open for 0% of the time, Pallas kernels for 4%

profile of v1, /device:TPU:31, one launch (start us, length us, event | category | flops | bytes accessed | tf_op | source)
XLA Modules:
  0.0 122.2 jit_solution(17186597016221202345)
XLA Ops:
  0.0 1.9 %slice.3.op_ref = bf16[768,1536]{1,0:T(8,128)(2,1)S(1)} slice(bf16[1536,1536]{1,0:T(8,128)(2,1)} %bitcast.6), slice={[0:768], [0:1536]} | slice | bytes 4718592 | tf_op jit(solution)/shard_map/slice | solution.py:287
  2.2 0.8 shard_map.29.turn_ref
  3.0 0.7 collective-permute-start.1
  4.2 1.1 shard_map.30.turn_ref.s_ref
  5.4 1.9 %collective-permute-done.mid_ref = bf16[768,256]{1,0:T(8,128)(2,1)S(1)} collective-permute-done((bf16[768,256]{1,0:T(8,128)(2,1)S(1)}, bf16[768,256]{1,0:T(8,128)(2,1)S(1)}, u32[]{:S(2)}, u32[]{:S(2)}) %collective-permute-start) | collective-permute-done | bytes 393248 | tf_op jit(solution)/shard_map/ppermute | solution.py:292
  7.5 0.7 collective-permute-start.8
  8.1 0.7 collective-permute-start.6
  8.8 0.7 collective-permute-start.7
  9.6 0.7 collective-permute-start.5
  10.2 0.7 collective-permute-start.3
  11.2 0.7 collective-permute-start.10
  11.9 0.7 collective-permute-start.4
  12.5 0.7 collective-permute-start.9
  13.2 0.7 collective-permute-start.12
  14.0 0.7 collective-permute-start.17
  14.7 0.7 collective-permute-start.15
  15.4 0.7 collective-permute-start.14
  16.1 0.7 collective-permute-start.16
  16.8 1.3 %collective-permute-start.11 = (bf16[512,128]{1,0:T(8,128)(2,1)S(1)}, bf16[512,128]{1,0:T(8,128)(2,1)S(1)}, u32[]{:S(2)}, u32[]{:S(2)}) collective-permute-start(bf16[512,128]{1,0:T(8,128)(2,1)S(1)} %get-tuple-element.108), channel_id=1, source_target_pairs={{4,6},{5,7},{18,20},{19,21},{28,30},{29,31}} | collective-permute-start | bytes 393224 | tf_op jit(solution)/shard_map/ppermute | solution.py:327
  18.1 0.7 collective-permute-start.13
  18.8 0.7 collective-permute-start.18
  19.5 0.7 collective-permute-start.19
  20.2 5.9 %collective-permute-done.11.refs_0_.refs_13_ = bf16[512,128]{1,0:T(8,128)(2,1)S(1)} collective-permute-done((bf16[512,128]{1,0:T(8,128)(2,1)S(1)}, bf16[512,128]{1,0:T(8,128)(2,1)S(1)}, u32[]{:S(2)}, u32[]{:S(2)}) %collective-permute-start.11) | collective-permute-done | bytes 131104 | tf_op jit(solution)/shard_map/ppermute | solution.py:327
  26.2 0.7 collective-permute-start.26
  26.9 0.7 collective-permute-start.21
  27.5 0.7 collective-permute-start.24
  28.2 1.3 %collective-permute-start.25 = (bf16[512,128]{1,0:T(8,128)(2,1)S(1)}, bf16[512,128]{1,0:T(8,128)(2,1)S(1)}, u32[]{:S(2)}, u32[]{:S(2)}) collective-permute-start(bf16[512,128]{1,0:T(8,128)(2,1)S(1)} %get-tuple-element.126), channel_id=1, source_target_pairs={{6,8},{7,9},{20,22},{21,23},{28,30},{29,31}} | collective-permute-start | bytes 393224 | tf_op jit(solution)/shard_map/ppermute | solution.py:327
  29.6 0.7 collective-permute-start.23
  30.3 11.2 %collective-permute-done.25.refs_0_.refs_1_.refs_19_ = bf16[512,128]{1,0:T(8,128)(2,1)S(1)} collective-permute-done((bf16[512,128]{1,0:T(8,128)(2,1)S(1)}, bf16[512,128]{1,0:T(8,128)(2,1)S(1)}, u32[]{:S(2)}, u32[]{:S(2)}) %collective-permute-start.25) | collective-permute-done | bytes 131104 | tf_op jit(solution)/shard_map/ppermute | solution.py:327
  42.3 1.3 %collective-permute-start.20 = (bf16[512,128]{1,0:T(8,128)(2,1)S(1)}, bf16[512,128]{1,0:T(8,128)(2,1)S(1)}, u32[]{:S(2)}, u32[]{:S(2)}) collective-permute-start(bf16[512,128]{1,0:T(8,128)(2,1)S(1)} %get-tuple-element.120), channel_id=1, source_target_pairs={{6,8},{7,9},{20,22},{21,23},{28,30},{29,31}} | collective-permute-start | bytes 393224 | tf_op jit(solution)/shard_map/ppermute | solution.py:327
  43.6 1.3 %collective-permute-start.22 = (bf16[512,128]{1,0:T(8,128)(2,1)S(1)}, bf16[512,128]{1,0:T(8,128)(2,1)S(1)}, u32[]{:S(2)}, u32[]{:S(2)}) collective-permute-start(bf16[512,128]{1,0:T(8,128)(2,1)S(1)} %get-tuple-element.123), channel_id=1, source_target_pairs={{6,8},{7,9},{20,22},{21,23},{28,30},{29,31}} | collective-permute-start | bytes 393224 | tf_op jit(solution)/shard_map/ppermute | solution.py:327
  44.9 0.7 collective-permute-start.27
  45.5 2.8 %collective-permute-done.20.refs_0_.refs_18_ = bf16[512,128]{1,0:T(8,128)(2,1)S(1)} collective-permute-done((bf16[512,128]{1,0:T(8,128)(2,1)S(1)}, bf16[512,128]{1,0:T(8,128)(2,1)S(1)}, u32[]{:S(2)}, u32[]{:S(2)}) %collective-permute-start.20) | collective-permute-done | bytes 131104 | tf_op jit(solution)/shard_map/ppermute | solution.py:327
  49.0 0.7 collective-permute-done.22.refs_0_.refs_1_.refs_19_
  49.7 1.5 %slice-done = s8[4194304]{0:T(1024)(128)(4,1)S(1)} async-done(((s8[4718592]{0:T(1024)(128)(4,1)}), s8[4194304]{0:T(1024)(128)(4,1)S(1)}, s32[]{:S(2)}) %slice-start) | async-done | bytes 4194328
  51.5 1.7 %shard_map.63 = (f32[768,1024]{1,0:T(8,128)S(1)}, f32[8,128]{1,0:T(8,128)S(1)}) custom-call(bf16[1536,1536]{1,0:T(8,128)(2,1)S(1)} %bitcast.9, bf16[768,1024]{1,0:T(8,128)(2,1)S(1)} %bitcast.17, bf16[1024,128]{1,0:T(8,128)(2,1)S(1)} %shard_map.62.turn_ref), custom_call_target="tpu_custom_call" | custom-call | tf_op jit(solution)/shard_map/pallas_call | solution.py:346
  53.2 0.7 collective-permute-start.35
  54.0 0.7 collective-permute-start.32
  54.7 0.7 collective-permute-start.33
  55.3 0.7 collective-permute-start.34
  56.0 0.7 collective-permute-start.29
  56.7 0.7 collective-permute-start.31
  57.5 0.7 collective-permute-start.37
  58.2 0.7 collective-permute-start.44
  58.9 0.7 collective-permute-start.36
  59.6 0.7 collective-permute-start.39
  61.0 0.7 collective-permute-start.43
  62.4 0.7 collective-permute-start.41
  63.2 1.3 %collective-permute-start.45 = (bf16[1024,128]{1,0:T(8,128)(2,1)S(1)}, bf16[1024,128]{1,0:T(8,128)(2,1)S(1)}, u32[]{:S(2)}, u32[]{:S(2)}) collective-permute-start(bf16[1024,128]{1,0:T(8,128)(2,1)S(1)} %shard_map.78.turn_ref), channel_id=1, source_target_pairs={{14,30},{15,31}} | collective-permute-start | bytes 786440 | tf_op jit(solution)/shard_map/ppermute | solution.py:342
  64.5 0.7 collective-permute-start.40
  65.1 1.3 %collective-permute-start.46 = (bf16[512,128]{1,0:T(8,128)(2,1)S(1)}, bf16[512,128]{1,0:T(8,128)(2,1)S(1)}, u32[]{:S(2)}, u32[]{:S(2)}) collective-permute-start(bf16[512,128]{1,0:T(8,128)(2,1)S(1)} %get-tuple-element.157), channel_id=1, source_target_pairs={{4,6},{5,7},{18,20},{19,21},{28,30},{29,31}} | collective-permute-start | bytes 393224 | tf_op jit(solution)/shard_map/ppermute | solution.py:327
  66.4 1.3 %collective-permute-start.47 = (bf16[512,128]{1,0:T(8,128)(2,1)S(1)}, bf16[512,128]{1,0:T(8,128)(2,1)S(1)}, u32[]{:S(2)}, u32[]{:S(2)}) collective-permute-start(bf16[512,128]{1,0:T(8,128)(2,1)S(1)} %get-tuple-element.158), channel_id=1, source_target_pairs={{6,8},{7,9},{20,22},{21,23},{28,30},{29,31}} | collective-permute-start | bytes 393224 | tf_op jit(solution)/shard_map/ppermute | solution.py:327
  67.8 19.2 %collective-permute-done.46.refs_38_ = bf16[512,128]{1,0:T(8,128)(2,1)S(1)} collective-permute-done((bf16[512,128]{1,0:T(8,128)(2,1)S(1)}, bf16[512,128]{1,0:T(8,128)(2,1)S(1)}, u32[]{:S(2)}, u32[]{:S(2)}) %collective-permute-start.46) | collective-permute-done | bytes 131104 | tf_op jit(solution)/shard_map/ppermute | solution.py:327
  87.0 1.4 %collective-permute-done.47.refs_39_ = bf16[512,128]{1,0:T(8,128)(2,1)S(1)} collective-permute-done((bf16[512,128]{1,0:T(8,128)(2,1)S(1)}, bf16[512,128]{1,0:T(8,128)(2,1)S(1)}, u32[]{:S(2)}, u32[]{:S(2)}) %collective-permute-start.47) | collective-permute-done | bytes 131104 | tf_op jit(solution)/shard_map/ppermute | solution.py:327
  88.4 5.2 %collective-permute-done.45.refs_37_ = bf16[1024,128]{1,0:T(8,128)(2,1)S(1)} collective-permute-done((bf16[1024,128]{1,0:T(8,128)(2,1)S(1)}, bf16[1024,128]{1,0:T(8,128)(2,1)S(1)}, u32[]{:S(2)}, u32[]{:S(2)}) %collective-permute-start.45) | collective-permute-done | bytes 262176 | tf_op jit(solution)/shard_map/ppermute | solution.py:342
  94.0 12.7 %collective-permute-start.48 = (bf16[768,256]{1,0:T(8,128)(2,1)S(1)}, bf16[768,256]{1,0:T(8,128)(2,1)S(1)}, u32[]{:S(2)}, u32[]{:S(2)}) collective-permute-start(bf16[768,256]{1,0:T(8,128)(2,1)S(1)} %get-tuple-element.159), channel_id=1, source_target_pairs={{0,1},{1,0},{2,3},{3,2},{4,5},{5,4},{6,7},{7,6},{8,9},{9,8},{10,11... | collective-permute-start | bytes 1179656 | tf_op jit(solution)/shard_map/ppermute | solution.py:363
  106.7 1.3 %collective-permute-start.49 = (bf16[1024,128]{1,0:T(8,128)(2,1)S(1)}, bf16[1024,128]{1,0:T(8,128)(2,1)S(1)}, u32[]{:S(2)}, u32[]{:S(2)}) collective-permute-start(bf16[1024,128]{1,0:T(8,128)(2,1)S(1)} %shard_map.81.turn_ref), channel_id=1, source_target_pairs={{14,30},{15,31}} | collective-permute-start | bytes 786440 | tf_op jit(solution)/shard_map/ppermute | solution.py:342
  108.0 1.3 %collective-permute-start.50 = (bf16[512,128]{1,0:T(8,128)(2,1)S(1)}, bf16[512,128]{1,0:T(8,128)(2,1)S(1)}, u32[]{:S(2)}, u32[]{:S(2)}) collective-permute-start(bf16[512,128]{1,0:T(8,128)(2,1)S(1)} %get-tuple-element.163), channel_id=1, source_target_pairs={{6,8},{7,9},{20,22},{21,23},{28,30},{29,31}} | collective-permute-start | bytes 393224 | tf_op jit(solution)/shard_map/ppermute | solution.py:327
  109.3 1.3 %collective-permute-start.51 = (bf16[512,128]{1,0:T(8,128)(2,1)S(1)}, bf16[512,128]{1,0:T(8,128)(2,1)S(1)}, u32[]{:S(2)}, u32[]{:S(2)}) collective-permute-start(bf16[512,128]{1,0:T(8,128)(2,1)S(1)} %get-tuple-element.164), channel_id=1, source_target_pairs={{6,8},{7,9},{20,22},{21,23},{28,30},{29,31}} | collective-permute-start | bytes 393224 | tf_op jit(solution)/shard_map/ppermute | solution.py:327
  111.6 3.3 %collective-permute-done.50.refs_38_ = bf16[512,128]{1,0:T(8,128)(2,1)S(1)} collective-permute-done((bf16[512,128]{1,0:T(8,128)(2,1)S(1)}, bf16[512,128]{1,0:T(8,128)(2,1)S(1)}, u32[]{:S(2)}, u32[]{:S(2)}) %collective-permute-start.50) | collective-permute-done | bytes 131104 | tf_op jit(solution)/shard_map/ppermute | solution.py:327
  114.9 2.8 %collective-permute-done.51.refs_39_ = bf16[512,128]{1,0:T(8,128)(2,1)S(1)} collective-permute-done((bf16[512,128]{1,0:T(8,128)(2,1)S(1)}, bf16[512,128]{1,0:T(8,128)(2,1)S(1)}, u32[]{:S(2)}, u32[]{:S(2)}) %collective-permute-start.51) | collective-permute-done | bytes 131104 | tf_op jit(solution)/shard_map/ppermute | solution.py:327
  118.1 0.9 collective-permute-start.52
  119.5 0.9 collective-permute-done.52.in_ref
  120.3 1.7 %shard_map.87 = bf16[768,1024]{1,0:T(8,128)(2,1)} custom-call(s32[1]{0:T(128)} %bitcast.3.parity_ref, bf16[1536,1536]{1,0:T(8,128)(2,1)S(1)} %bitcast.13, f32[768,1024]{1,0:T(8,128)S(1)} %get-tuple-element.131.r_ref, bf16[768,256]{1,0:T(8,128)(2,1)S(1)} %collective-permute-done.52.in_ref, f32[8,128]{1,0:T(8,128)S(1)} %get-tuple-element.167.turn_ref, ...), custom_call_target="tpu_custom_call" | custom-call | tf_op jit(solution)/shard_map/pallas_call | solution.py:367
  (110 shorter events, 6.7 us)
Async XLA Ops:
  0.0 2.1 %copy-start = (bf16[1,1,1,768,1024]{4,3,2,1,0:T(8,128)(2,1)S(1)}, bf16[1,1,1,768,1024]{4,3,2,1,0:T(8,128)(2,1)}, u32[]{:S(2)}) copy-start(bf16[1,1,1,768,1024]{4,3,2,1,0:T(8,128)(2,1)} %param.3) | copy-start | bytes 4718596
  3.0 4.4 %collective-permute-start.1 = (bf16[768,512]{1,0:T(8,128)(2,1)S(1)}, bf16[768,512]{1,0:T(8,128)(2,1)S(1)}, u32[]{:S(2)}, u32[]{:S(2)}) collective-permute-start(bf16[768,512]{1,0:T(8,128)(2,1)S(1)} %shard_map.29.turn_ref), channel_id=1, source_target_pairs={{0,1},{1,0},{2,3},{3,2},{4,5},{5,4},{6,7},{7,6},{8,9},{9,8},{10,11... | collective-permute-start | bytes 2359304 | tf_op jit(solution)/shard_map/ppermute | solution.py:296
  3.7 6.5 %collective-permute-start.2 = (bf16[768,512]{1,0:T(8,128)(2,1)S(1)}, bf16[768,512]{1,0:T(8,128)(2,1)S(1)}, u32[]{:S(2)}, u32[]{:S(2)}) collective-permute-start(bf16[768,512]{1,0:T(8,128)(2,1)S(1)} %get-tuple-element.98), channel_id=1, source_target_pairs={{0,1},{1,0},{2,3},{3,2},{4,5},{5,4},{6,7},{7,6},{8,9},{9,8},{10,11... | collective-permute-start | bytes 2359304 | tf_op jit(solution)/shard_map/ppermute | solution.py:297
  3.8 3.5 %collective-permute-start = (bf16[768,256]{1,0:T(8,128)(2,1)S(1)}, bf16[768,256]{1,0:T(8,128)(2,1)S(1)}, u32[]{:S(2)}, u32[]{:S(2)}) collective-permute-start(bf16[768,256]{1,0:T(8,128)(2,1)S(1)} %get-tuple-element.93.turn_ref), channel_id=1, source_target_pairs={{0,1},{1,0},{2,3},{3,2},{4,5},{5,4},{6,7},{7,6},{8,9},{9,8},{10,11... | collective-permute-start | bytes 1179656 | tf_op jit(solution)/shard_map/ppermute | solution.py:292
  7.5 3.6 %collective-permute-start.8 = (bf16[1024,128]{1,0:T(8,128)(2,1)S(1)}, bf16[1024,128]{1,0:T(8,128)(2,1)S(1)}, u32[]{:S(2)}, u32[]{:S(2)}) collective-permute-start(bf16[1024,128]{1,0:T(8,128)(2,1)S(1)} %shard_map.34.turn_ref), channel_id=1, source_target_pairs={{0,16},{1,17}} | collective-permute-start | bytes 786440 | tf_op jit(solution)/shard_map/ppermute | solution.py:342
  8.1 3.0 %collective-permute-start.6 = (bf16[512,128]{1,0:T(8,128)(2,1)S(1)}, bf16[512,128]{1,0:T(8,128)(2,1)S(1)}, u32[]{:S(2)}, u32[]{:S(2)}) collective-permute-start(bf16[512,128]{1,0:T(8,128)(2,1)S(1)} %get-tuple-element.101), channel_id=1, source_target_pairs={{0,2},{1,3},{10,12},{11,13},{24,26},{25,27}} | collective-permute-start | bytes 393224 | tf_op jit(solution)/shard_map/ppermute | solution.py:327
  8.8 2.3 %collective-permute-start.7 = (bf16[512,128]{1,0:T(8,128)(2,1)S(1)}, bf16[512,128]{1,0:T(8,128)(2,1)S(1)}, u32[]{:S(2)}, u32[]{:S(2)}) collective-permute-start(bf16[512,128]{1,0:T(8,128)(2,1)S(1)} %get-tuple-element.102), channel_id=1, source_target_pairs={{0,2},{1,3},{8,10},{9,11},{22,24},{23,25}} | collective-permute-start | bytes 393224 | tf_op jit(solution)/shard_map/ppermute | solution.py:327
  9.6 4.4 %collective-permute-start.5 = (bf16[1024,128]{1,0:T(8,128)(2,1)S(1)}, bf16[1024,128]{1,0:T(8,128)(2,1)S(1)}, u32[]{:S(2)}, u32[]{:S(2)}) collective-permute-start(bf16[1024,128]{1,0:T(8,128)(2,1)S(1)} %shard_map.37.turn_ref), channel_id=1, source_target_pairs={{0,16},{1,17}} | collective-permute-start | bytes 786440 | tf_op jit(solution)/shard_map/ppermute | solution.py:342
  10.2 3.0 %collective-permute-start.3 = (bf16[512,128]{1,0:T(8,128)(2,1)S(1)}, bf16[512,128]{1,0:T(8,128)(2,1)S(1)}, u32[]{:S(2)}, u32[]{:S(2)}) collective-permute-start(bf16[512,128]{1,0:T(8,128)(2,1)S(1)} %get-tuple-element.99), channel_id=1, source_target_pairs={{0,2},{1,3},{8,10},{9,11},{22,24},{23,25}} | collective-permute-start | bytes 393224 | tf_op jit(solution)/shard_map/ppermute | solution.py:327
  11.2 4.2 %collective-permute-start.10 = (bf16[1024,128]{1,0:T(8,128)(2,1)S(1)}, bf16[1024,128]{1,0:T(8,128)(2,1)S(1)}, u32[]{:S(2)}, u32[]{:S(2)}) collective-permute-start(bf16[1024,128]{1,0:T(8,128)(2,1)S(1)} %shard_map.41.turn_ref), channel_id=1, source_target_pairs={{2,18},{3,19}} | collective-permute-start | bytes 786440 | tf_op jit(solution)/shard_map/ppermute | solution.py:342
  11.9 2.1 %collective-permute-start.4 = (bf16[512,128]{1,0:T(8,128)(2,1)S(1)}, bf16[512,128]{1,0:T(8,128)(2,1)S(1)}, u32[]{:S(2)}, u32[]{:S(2)}) collective-permute-start(bf16[512,128]{1,0:T(8,128)(2,1)S(1)} %get-tuple-element.100), channel_id=1, source_target_pairs={{0,2},{1,3},{8,10},{9,11},{22,24},{23,25}} | collective-permute-start | bytes 393224 | tf_op jit(solution)/shard_map/ppermute | solution.py:327
  12.5 2.8 %collective-permute-start.9 = (bf16[512,128]{1,0:T(8,128)(2,1)S(1)}, bf16[512,128]{1,0:T(8,128)(2,1)S(1)}, u32[]{:S(2)}, u32[]{:S(2)}) collective-permute-start(bf16[512,128]{1,0:T(8,128)(2,1)S(1)} %get-tuple-element.107), channel_id=1, source_target_pairs={{2,4},{3,5},{12,14},{13,15},{16,18},{17,19},{26,28},{27,29}} | collective-permute-start | bytes 393224 | tf_op jit(solution)/shard_map/ppermute | solution.py:327
  13.2 2.2 %collective-permute-start.12 = (bf16[512,128]{1,0:T(8,128)(2,1)S(1)}, bf16[512,128]{1,0:T(8,128)(2,1)S(1)}, u32[]{:S(2)}, u32[]{:S(2)}) collective-permute-start(bf16[512,128]{1,0:T(8,128)(2,1)S(1)} %get-tuple-element.110), channel_id=1, source_target_pairs={{2,4},{3,5},{10,12},{11,13},{16,18},{17,19},{24,26},{25,27}} | collective-permute-start | bytes 393224 | tf_op jit(solution)/shard_map/ppermute | solution.py:327
  14.0 4.8 %collective-permute-start.17 = (bf16[1024,128]{1,0:T(8,128)(2,1)S(1)}, bf16[1024,128]{1,0:T(8,128)(2,1)S(1)}, u32[]{:S(2)}, u32[]{:S(2)}) collective-permute-start(bf16[1024,128]{1,0:T(8,128)(2,1)S(1)} %shard_map.44.turn_ref), channel_id=1, source_target_pairs={{2,18},{3,19}} | collective-permute-start | bytes 786440 | tf_op jit(solution)/shard_map/ppermute | solution.py:342
  14.7 3.4 %collective-permute-start.15 = (bf16[512,128]{1,0:T(8,128)(2,1)S(1)}, bf16[512,128]{1,0:T(8,128)(2,1)S(1)}, u32[]{:S(2)}, u32[]{:S(2)}) collective-permute-start(bf16[512,128]{1,0:T(8,128)(2,1)S(1)} %get-tuple-element.113), channel_id=1, source_target_pairs={{2,4},{3,5},{10,12},{11,13},{16,18},{17,19},{24,26},{25,27}} | collective-permute-start | bytes 393224 | tf_op jit(solution)/shard_map/ppermute | solution.py:327
  15.4 10.7 %collective-permute-start.14 = (bf16[1024,128]{1,0:T(8,128)(2,1)S(1)}, bf16[1024,128]{1,0:T(8,128)(2,1)S(1)}, u32[]{:S(2)}, u32[]{:S(2)}) collective-permute-start(bf16[1024,128]{1,0:T(8,128)(2,1)S(1)} %shard_map.47.turn_ref), channel_id=1, source_target_pairs={{4,20},{5,21}} | collective-permute-start | bytes 786440 | tf_op jit(solution)/shard_map/ppermute | solution.py:342
  16.1 3.4 %collective-permute-start.16 = (bf16[512,128]{1,0:T(8,128)(2,1)S(1)}, bf16[512,128]{1,0:T(8,128)(2,1)S(1)}, u32[]{:S(2)}, u32[]{:S(2)}) collective-permute-start(bf16[512,128]{1,0:T(8,128)(2,1)S(1)} %get-tuple-element.114), channel_id=1, source_target_pairs={{2,4},{3,5},{10,12},{11,13},{16,18},{17,19},{24,26},{25,27}} | collective-permute-start | bytes 393224 | tf_op jit(solution)/shard_map/ppermute | solution.py:327
  16.8 9.3 %collective-permute-start.11 = (bf16[512,128]{1,0:T(8,128)(2,1)S(1)}, bf16[512,128]{1,0:T(8,128)(2,1)S(1)}, u32[]{:S(2)}, u32[]{:S(2)}) collective-permute-start(bf16[512,128]{1,0:T(8,128)(2,1)S(1)} %get-tuple-element.108), channel_id=1, source_target_pairs={{4,6},{5,7},{18,20},{19,21},{28,30},{29,31}} | collective-permute-start | bytes 393224 | tf_op jit(solution)/shard_map/ppermute | solution.py:327
  18.1 8.0 %collective-permute-start.13 = (bf16[512,128]{1,0:T(8,128)(2,1)S(1)}, bf16[512,128]{1,0:T(8,128)(2,1)S(1)}, u32[]{:S(2)}, u32[]{:S(2)}) collective-permute-start(bf16[512,128]{1,0:T(8,128)(2,1)S(1)} %get-tuple-element.111), channel_id=1, source_target_pairs={{4,6},{5,7},{12,14},{13,15},{18,20},{19,21},{26,28},{27,29}} | collective-permute-start | bytes 393224 | tf_op jit(solution)/shard_map/ppermute | solution.py:327
  18.8 9.4 %collective-permute-start.18 = (bf16[512,128]{1,0:T(8,128)(2,1)S(1)}, bf16[512,128]{1,0:T(8,128)(2,1)S(1)}, u32[]{:S(2)}, u32[]{:S(2)}) collective-permute-start(bf16[512,128]{1,0:T(8,128)(2,1)S(1)} %get-tuple-element.119), channel_id=1, source_target_pairs={{4,6},{5,7},{12,14},{13,15},{18,20},{19,21},{26,28},{27,29}} | collective-permute-start | bytes 393224 | tf_op jit(solution)/shard_map/ppermute | solution.py:327
  19.5 10.0 %collective-permute-start.19 = (bf16[1024,128]{1,0:T(8,128)(2,1)S(1)}, bf16[1024,128]{1,0:T(8,128)(2,1)S(1)}, u32[]{:S(2)}, u32[]{:S(2)}) collective-permute-start(bf16[1024,128]{1,0:T(8,128)(2,1)S(1)} %shard_map.50.turn_ref), channel_id=1, source_target_pairs={{4,20},{5,21}} | collective-permute-start | bytes 786440 | tf_op jit(solution)/shard_map/ppermute | solution.py:342
  26.2 4.1 %collective-permute-start.26 = (bf16[1024,128]{1,0:T(8,128)(2,1)S(1)}, bf16[1024,128]{1,0:T(8,128)(2,1)S(1)}, u32[]{:S(2)}, u32[]{:S(2)}) collective-permute-start(bf16[1024,128]{1,0:T(8,128)(2,1)S(1)} %shard_map.53.turn_ref), channel_id=1, source_target_pairs={{6,22},{7,23}} | collective-permute-start | bytes 786440 | tf_op jit(solution)/shard_map/ppermute | solution.py:342
  26.9 2.7 %collective-permute-start.21 = (bf16[512,128]{1,0:T(8,128)(2,1)S(1)}, bf16[512,128]{1,0:T(8,128)(2,1)S(1)}, u32[]{:S(2)}, u32[]{:S(2)}) collective-permute-start(bf16[512,128]{1,0:T(8,128)(2,1)S(1)} %get-tuple-element.122), channel_id=1, source_target_pairs={{4,6},{5,7},{12,14},{13,15},{18,20},{19,21},{26,28},{27,29}} | collective-permute-start | bytes 393224 | tf_op jit(solution)/shard_map/ppermute | solution.py:327
  27.5 2.8 %collective-permute-start.24 = (bf16[512,128]{1,0:T(8,128)(2,1)S(1)}, bf16[512,128]{1,0:T(8,128)(2,1)S(1)}, u32[]{:S(2)}, u32[]{:S(2)}) collective-permute-start(bf16[512,128]{1,0:T(8,128)(2,1)S(1)} %get-tuple-element.125), channel_id=1, source_target_pairs={{6,8},{7,9},{20,22},{21,23}} | collective-permute-start | bytes 393224 | tf_op jit(solution)/shard_map/ppermute | solution.py:327
  28.2 13.3 %collective-permute-start.25 = (bf16[512,128]{1,0:T(8,128)(2,1)S(1)}, bf16[512,128]{1,0:T(8,128)(2,1)S(1)}, u32[]{:S(2)}, u32[]{:S(2)}) collective-permute-start(bf16[512,128]{1,0:T(8,128)(2,1)S(1)} %get-tuple-element.126), channel_id=1, source_target_pairs={{6,8},{7,9},{20,22},{21,23},{28,30},{29,31}} | collective-permute-start | bytes 393224 | tf_op jit(solution)/shard_map/ppermute | solution.py:327
  29.6 19.4 %collective-permute-start.23 = (bf16[1024,128]{1,0:T(8,128)(2,1)S(1)}, bf16[1024,128]{1,0:T(8,128)(2,1)S(1)}, u32[]{:S(2)}, u32[]{:S(2)}) collective-permute-start(bf16[1024,128]{1,0:T(8,128)(2,1)S(1)} %shard_map.56.turn_ref), channel_id=1, source_target_pairs={{6,22},{7,23}} | collective-permute-start | bytes 786440 | tf_op jit(solution)/shard_map/ppermute | solution.py:342
  41.6 12.3 %collective-permute-start.28 = (bf16[1024,128]{1,0:T(8,128)(2,1)S(1)}, bf16[1024,128]{1,0:T(8,128)(2,1)S(1)}, u32[]{:S(2)}, u32[]{:S(2)}) collective-permute-start(bf16[1024,128]{1,0:T(8,128)(2,1)S(1)} %shard_map.59.turn_ref), channel_id=1, source_target_pairs={{8,24},{9,25}} | collective-permute-start | bytes 786440 | tf_op jit(solution)/shard_map/ppermute | solution.py:342
  42.3 6.1 %collective-permute-start.20 = (bf16[512,128]{1,0:T(8,128)(2,1)S(1)}, bf16[512,128]{1,0:T(8,128)(2,1)S(1)}, u32[]{:S(2)}, u32[]{:S(2)}) collective-permute-start(bf16[512,128]{1,0:T(8,128)(2,1)S(1)} %get-tuple-element.120), channel_id=1, source_target_pairs={{6,8},{7,9},{20,22},{21,23},{28,30},{29,31}} | collective-permute-start | bytes 393224 | tf_op jit(solution)/shard_map/ppermute | solution.py:327
  43.6 6.2 %collective-permute-start.22 = (bf16[512,128]{1,0:T(8,128)(2,1)S(1)}, bf16[512,128]{1,0:T(8,128)(2,1)S(1)}, u32[]{:S(2)}, u32[]{:S(2)}) collective-permute-start(bf16[512,128]{1,0:T(8,128)(2,1)S(1)} %get-tuple-element.123), channel_id=1, source_target_pairs={{6,8},{7,9},{20,22},{21,23},{28,30},{29,31}} | collective-permute-start | bytes 393224 | tf_op jit(solution)/shard_map/ppermute | solution.py:327
  44.9 9.0 %collective-permute-start.27 = (bf16[512,128]{1,0:T(8,128)(2,1)S(1)}, bf16[512,128]{1,0:T(8,128)(2,1)S(1)}, u32[]{:S(2)}, u32[]{:S(2)}) collective-permute-start(bf16[512,128]{1,0:T(8,128)(2,1)S(1)} %get-tuple-element.133), channel_id=1, source_target_pairs={{8,10},{9,11},{22,24},{23,25}} | collective-permute-start | bytes 393224 | tf_op jit(solution)/shard_map/ppermute | solution.py:327
  48.3 5.6 %collective-permute-start.30 = (bf16[512,128]{1,0:T(8,128)(2,1)S(1)}, bf16[512,128]{1,0:T(8,128)(2,1)S(1)}, u32[]{:S(2)}, u32[]{:S(2)}) collective-permute-start(bf16[512,128]{1,0:T(8,128)(2,1)S(1)} %get-tuple-element.136), channel_id=1, source_target_pairs={{0,2},{1,3},{8,10},{9,11},{22,24},{23,25}} | collective-permute-start | bytes 393224 | tf_op jit(solution)/shard_map/ppermute | solution.py:327
  49.0 2.2 %slice-start = ((s8[4718592]{0:T(1024)(128)(4,1)}), s8[4194304]{0:T(1024)(128)(4,1)S(1)}, s32[]{:S(2)}) async-start(s8[4718592]{0:T(1024)(128)(4,1)} %bitcast.7), calls=%async_computation | async-start | bytes 8388608
  49.7 1.7 %slice-start.1 = ((s8[4718592]{0:T(1024)(128)(4,1)}), s8[524288]{0:T(1024)(128)(4,1)S(1)}, s32[]{:S(2)}) async-start(s8[4718592]{0:T(1024)(128)(4,1)} %bitcast.7), calls=%async_computation.1 | async-start | bytes 1048576
  53.2 4.2 %collective-permute-start.35 = (bf16[1024,128]{1,0:T(8,128)(2,1)S(1)}, bf16[1024,128]{1,0:T(8,128)(2,1)S(1)}, u32[]{:S(2)}, u32[]{:S(2)}) collective-permute-start(bf16[1024,128]{1,0:T(8,128)(2,1)S(1)} %shard_map.62.turn_ref), channel_id=1, source_target_pairs={{8,24},{9,25}} | collective-permute-start | bytes 786440 | tf_op jit(solution)/shard_map/ppermute | solution.py:342
  54.0 4.2 %collective-permute-start.32 = (bf16[1024,128]{1,0:T(8,128)(2,1)S(1)}, bf16[1024,128]{1,0:T(8,128)(2,1)S(1)}, u32[]{:S(2)}, u32[]{:S(2)}) collective-permute-start(bf16[1024,128]{1,0:T(8,128)(2,1)S(1)} %shard_map.66.turn_ref), channel_id=1, source_target_pairs={{10,26},{11,27}} | collective-permute-start | bytes 786440 | tf_op jit(solution)/shard_map/ppermute | solution.py:342
  54.7 2.0 %collective-permute-start.33 = (bf16[512,128]{1,0:T(8,128)(2,1)S(1)}, bf16[512,128]{1,0:T(8,128)(2,1)S(1)}, u32[]{:S(2)}, u32[]{:S(2)}) collective-permute-start(bf16[512,128]{1,0:T(8,128)(2,1)S(1)} %get-tuple-element.139), channel_id=1, source_target_pairs={{0,2},{1,3},{8,10},{9,11},{22,24},{23,25}} | collective-permute-start | bytes 393224 | tf_op jit(solution)/shard_map/ppermute | solution.py:327
  55.3 2.1 %collective-permute-start.34 = (bf16[512,128]{1,0:T(8,128)(2,1)S(1)}, bf16[512,128]{1,0:T(8,128)(2,1)S(1)}, u32[]{:S(2)}, u32[]{:S(2)}) collective-permute-start(bf16[512,128]{1,0:T(8,128)(2,1)S(1)} %get-tuple-element.140), channel_id=1, source_target_pairs={{0,2},{1,3},{8,10},{9,11},{22,24},{23,25}} | collective-permute-start | bytes 393224 | tf_op jit(solution)/shard_map/ppermute | solution.py:327
  56.0 2.1 %collective-permute-start.29 = (bf16[512,128]{1,0:T(8,128)(2,1)S(1)}, bf16[512,128]{1,0:T(8,128)(2,1)S(1)}, u32[]{:S(2)}, u32[]{:S(2)}) collective-permute-start(bf16[512,128]{1,0:T(8,128)(2,1)S(1)} %get-tuple-element.134), channel_id=1, source_target_pairs={{0,2},{1,3},{10,12},{11,13},{24,26},{25,27}} | collective-permute-start | bytes 393224 | tf_op jit(solution)/shard_map/ppermute | solution.py:327
  56.7 1.5 %collective-permute-start.31 = (bf16[512,128]{1,0:T(8,128)(2,1)S(1)}, bf16[512,128]{1,0:T(8,128)(2,1)S(1)}, u32[]{:S(2)}, u32[]{:S(2)}) collective-permute-start(bf16[512,128]{1,0:T(8,128)(2,1)S(1)} %get-tuple-element.137), channel_id=1, source_target_pairs={{2,4},{3,5},{10,12},{11,13},{16,18},{17,19},{24,26},{25,27}} | collective-permute-start | bytes 393224 | tf_op jit(solution)/shard_map/ppermute | solution.py:327
  57.5 4.2 %collective-permute-start.37 = (bf16[1024,128]{1,0:T(8,128)(2,1)S(1)}, bf16[1024,128]{1,0:T(8,128)(2,1)S(1)}, u32[]{:S(2)}, u32[]{:S(2)}) collective-permute-start(bf16[1024,128]{1,0:T(8,128)(2,1)S(1)} %shard_map.69.turn_ref), channel_id=1, source_target_pairs={{10,26},{11,27}} | collective-permute-start | bytes 786440 | tf_op jit(solution)/shard_map/ppermute | solution.py:342
  58.2 4.9 %collective-permute-start.44 = (bf16[1024,128]{1,0:T(8,128)(2,1)S(1)}, bf16[1024,128]{1,0:T(8,128)(2,1)S(1)}, u32[]{:S(2)}, u32[]{:S(2)}) collective-permute-start(bf16[1024,128]{1,0:T(8,128)(2,1)S(1)} %shard_map.72.turn_ref), channel_id=1, source_target_pairs={{12,28},{13,29}} | collective-permute-start | bytes 786440 | tf_op jit(solution)/shard_map/ppermute | solution.py:342
  58.9 2.0 %collective-permute-start.36 = (bf16[512,128]{1,0:T(8,128)(2,1)S(1)}, bf16[512,128]{1,0:T(8,128)(2,1)S(1)}, u32[]{:S(2)}, u32[]{:S(2)}) collective-permute-start(bf16[512,128]{1,0:T(8,128)(2,1)S(1)} %get-tuple-element.145), channel_id=1, source_target_pairs={{2,4},{3,5},{10,12},{11,13},{16,18},{17,19},{24,26},{25,27}} | collective-permute-start | bytes 393224 | tf_op jit(solution)/shard_map/ppermute | solution.py:327
  59.6 2.8 %collective-permute-start.39 = (bf16[512,128]{1,0:T(8,128)(2,1)S(1)}, bf16[512,128]{1,0:T(8,128)(2,1)S(1)}, u32[]{:S(2)}, u32[]{:S(2)}) collective-permute-start(bf16[512,128]{1,0:T(8,128)(2,1)S(1)} %get-tuple-element.148), channel_id=1, source_target_pairs={{2,4},{3,5},{10,12},{11,13},{16,18},{17,19},{24,26},{25,27}} | collective-permute-start | bytes 393224 | tf_op jit(solution)/shard_map/ppermute | solution.py:327
  60.3 2.8 %collective-permute-start.42 = (bf16[512,128]{1,0:T(8,128)(2,1)S(1)}, bf16[512,128]{1,0:T(8,128)(2,1)S(1)}, u32[]{:S(2)}, u32[]{:S(2)}) collective-permute-start(bf16[512,128]{1,0:T(8,128)(2,1)S(1)} %get-tuple-element.151), channel_id=1, source_target_pairs={{2,4},{3,5},{12,14},{13,15},{16,18},{17,19},{26,28},{27,29}} | collective-permute-start | bytes 393224 | tf_op jit(solution)/shard_map/ppermute | solution.py:327
  61.0 2.2 %collective-permute-start.43 = (bf16[512,128]{1,0:T(8,128)(2,1)S(1)}, bf16[512,128]{1,0:T(8,128)(2,1)S(1)}, u32[]{:S(2)}, u32[]{:S(2)}) collective-permute-start(bf16[512,128]{1,0:T(8,128)(2,1)S(1)} %get-tuple-element.152), channel_id=1, source_target_pairs={{4,6},{5,7},{12,14},{13,15},{18,20},{19,21},{26,28},{27,29}} | collective-permute-start | bytes 393224 | tf_op jit(solution)/shard_map/ppermute | solution.py:327
  61.7 4.8 %collective-permute-start.38 = (bf16[512,128]{1,0:T(8,128)(2,1)S(1)}, bf16[512,128]{1,0:T(8,128)(2,1)S(1)}, u32[]{:S(2)}, u32[]{:S(2)}) collective-permute-start(bf16[512,128]{1,0:T(8,128)(2,1)S(1)} %get-tuple-element.146), channel_id=1, source_target_pairs={{4,6},{5,7},{12,14},{13,15},{18,20},{19,21},{26,28},{27,29}} | collective-permute-start | bytes 393224 | tf_op jit(solution)/shard_map/ppermute | solution.py:327
  62.4 5.4 %collective-permute-start.41 = (bf16[1024,128]{1,0:T(8,128)(2,1)S(1)}, bf16[1024,128]{1,0:T(8,128)(2,1)S(1)}, u32[]{:S(2)}, u32[]{:S(2)}) collective-permute-start(bf16[1024,128]{1,0:T(8,128)(2,1)S(1)} %shard_map.75.turn_ref), channel_id=1, source_target_pairs={{12,28},{13,29}} | collective-permute-start | bytes 786440 | tf_op jit(solution)/shard_map/ppermute | solution.py:342
  63.2 30.5 %collective-permute-start.45 = (bf16[1024,128]{1,0:T(8,128)(2,1)S(1)}, bf16[1024,128]{1,0:T(8,128)(2,1)S(1)}, u32[]{:S(2)}, u32[]{:S(2)}) collective-permute-start(bf16[1024,128]{1,0:T(8,128)(2,1)S(1)} %shard_map.78.turn_ref), channel_id=1, source_target_pairs={{14,30},{15,31}} | collective-permute-start | bytes 786440 | tf_op jit(solution)/shard_map/ppermute | solution.py:342
  64.5 3.3 %collective-permute-start.40 = (bf16[512,128]{1,0:T(8,128)(2,1)S(1)}, bf16[512,128]{1,0:T(8,128)(2,1)S(1)}, u32[]{:S(2)}, u32[]{:S(2)}) collective-permute-start(bf16[512,128]{1,0:T(8,128)(2,1)S(1)} %get-tuple-element.149), channel_id=1, source_target_pairs={{4,6},{5,7},{12,14},{13,15},{18,20},{19,21},{26,28},{27,29}} | collective-permute-start | bytes 393224 | tf_op jit(solution)/shard_map/ppermute | solution.py:327
  65.1 21.8 %collective-permute-start.46 = (bf16[512,128]{1,0:T(8,128)(2,1)S(1)}, bf16[512,128]{1,0:T(8,128)(2,1)S(1)}, u32[]{:S(2)}, u32[]{:S(2)}) collective-permute-start(bf16[512,128]{1,0:T(8,128)(2,1)S(1)} %get-tuple-element.157), channel_id=1, source_target_pairs={{4,6},{5,7},{18,20},{19,21},{28,30},{29,31}} | collective-permute-start | bytes 393224 | tf_op jit(solution)/shard_map/ppermute | solution.py:327
  66.4 21.9 %collective-permute-start.47 = (bf16[512,128]{1,0:T(8,128)(2,1)S(1)}, bf16[512,128]{1,0:T(8,128)(2,1)S(1)}, u32[]{:S(2)}, u32[]{:S(2)}) collective-permute-start(bf16[512,128]{1,0:T(8,128)(2,1)S(1)} %get-tuple-element.158), channel_id=1, source_target_pairs={{6,8},{7,9},{20,22},{21,23},{28,30},{29,31}} | collective-permute-start | bytes 393224 | tf_op jit(solution)/shard_map/ppermute | solution.py:327
  94.0 17.1 %collective-permute-start.48 = (bf16[768,256]{1,0:T(8,128)(2,1)S(1)}, bf16[768,256]{1,0:T(8,128)(2,1)S(1)}, u32[]{:S(2)}, u32[]{:S(2)}) collective-permute-start(bf16[768,256]{1,0:T(8,128)(2,1)S(1)} %get-tuple-element.159), channel_id=1, source_target_pairs={{0,1},{1,0},{2,3},{3,2},{4,5},{5,4},{6,7},{7,6},{8,9},{9,8},{10,11... | collective-permute-start | bytes 1179656 | tf_op jit(solution)/shard_map/ppermute | solution.py:363
  106.7 11.1 %collective-permute-start.49 = (bf16[1024,128]{1,0:T(8,128)(2,1)S(1)}, bf16[1024,128]{1,0:T(8,128)(2,1)S(1)}, u32[]{:S(2)}, u32[]{:S(2)}) collective-permute-start(bf16[1024,128]{1,0:T(8,128)(2,1)S(1)} %shard_map.81.turn_ref), channel_id=1, source_target_pairs={{14,30},{15,31}} | collective-permute-start | bytes 786440 | tf_op jit(solution)/shard_map/ppermute | solution.py:342
  108.0 6.9 %collective-permute-start.50 = (bf16[512,128]{1,0:T(8,128)(2,1)S(1)}, bf16[512,128]{1,0:T(8,128)(2,1)S(1)}, u32[]{:S(2)}, u32[]{:S(2)}) collective-permute-start(bf16[512,128]{1,0:T(8,128)(2,1)S(1)} %get-tuple-element.163), channel_id=1, source_target_pairs={{6,8},{7,9},{20,22},{21,23},{28,30},{29,31}} | collective-permute-start | bytes 393224 | tf_op jit(solution)/shard_map/ppermute | solution.py:327
  109.3 8.4 %collective-permute-start.51 = (bf16[512,128]{1,0:T(8,128)(2,1)S(1)}, bf16[512,128]{1,0:T(8,128)(2,1)S(1)}, u32[]{:S(2)}, u32[]{:S(2)}) collective-permute-start(bf16[512,128]{1,0:T(8,128)(2,1)S(1)} %get-tuple-element.164), channel_id=1, source_target_pairs={{6,8},{7,9},{20,22},{21,23},{28,30},{29,31}} | collective-permute-start | bytes 393224 | tf_op jit(solution)/shard_map/ppermute | solution.py:327
  118.1 2.2 %collective-permute-start.52 = (bf16[768,256]{1,0:T(8,128)(2,1)S(1)}, bf16[768,256]{1,0:T(8,128)(2,1)S(1)}, u32[]{:S(2)}, u32[]{:S(2)}) collective-permute-start(bf16[768,256]{1,0:T(8,128)(2,1)S(1)} %get-tuple-element.165), channel_id=1, source_target_pairs={{0,1},{1,0},{2,3},{3,2},{4,5},{5,4},{6,7},{7,6},{8,9},{9,8},{10,11... | collective-permute-start | bytes 1179656 | tf_op jit(solution)/shard_map/ppermute | solution.py:363

commit v2 on v1

--- a/solution.py
+++ b/solution.py
@@ -147,11 +147,12 @@
         za, zb = paired(z_in, trace, slot)
         ya = None if y_in is None else y_in[...]
         upper = slice(0, 2 * trace)
-        sa, sb = pair_sources(parity_ref, s_ref, given_ref, upper, columns)
+        wanted = slice(0, (1 + has_row) * trace)
+        sa, _ = pair_sources(parity_ref, s_ref, given_ref, upper, columns)
+        _, sb = pair_sources(parity_ref, s_ref, given_ref, wanted, columns)
         a = lower_side(both_ref.at[0], upper, trace, sa, (xa, ya, za)).astype(bf16)
         mid = a[trace:]
-        wanted = slice(0, (1 + has_row) * trace)
-        b = lower_side(both_ref.at[1], wanted, trace, sb[wanted], (xb, None, zb))
+        b = lower_side(both_ref.at[1], wanted, trace, sb, (xb, None, zb))
         b = lower_side(both_ref.at[1], wanted, trace, b, (None, mid, None)).astype(bf16)
         x_out[:trace, :] = a[:trace]
         x_out[trace:, :] = b[:trace]

time: 123 us -> 123 us (level)
  no operation moved by 1% of the time
where the time goes in v2:
time: 123 us; the launch traced here: 122 us
  waiting for transfers between devices  55.6 us (45%)
  starting transfers between devices  53.2 us (43%)
  Pallas kernels  8.23 us (7%)
  local copies, waits for them, and re-layouts  3.86 us (3%)
  between operations  1.28 us (1%)
    ppermute x32, waiting for transfers between devices, shards(): lax.ppermute(sent[0], AXES, route(sizes, 1, tick, REPEAT[1][n]))  47.4 us
    ppermute x32, starting transfers between devices, shards(): lax.ppermute(sent[0], AXES, route(sizes, 1, tick, REPEAT[1][n]))  26.4 us
    ppermute x2, starting transfers between devices, shards(): back = lax.ppermute(other, 'gy', swap)  13.6 us
    ppermute x16, starting transfers between devices, shards(): lax.ppermute(turn, AXES, route(sizes, 0, tick, REPEAT[0]))  12 us
    ppermute x16, waiting for transfers between devices, shards(): lax.ppermute(turn, AXES, route(sizes, 0, tick, REPEAT[0]))  5.4 us
  transfers between devices with their start and end apart: 53, of which 12 were waited for; matrix products, arithmetic and copies ran while one was open for 0% of the time, Pallas kernels for 4%

profile of v2, /device:TPU:31, one launch (start us, length us, event | category | flops | bytes accessed | tf_op | source)
XLA Modules:
  0.0 122.2 jit_solution(13416379211079694683)
XLA Ops:
  0.0 1.9 %slice.3.op_ref = bf16[768,1536]{1,0:T(8,128)(2,1)S(1)} slice(bf16[1536,1536]{1,0:T(8,128)(2,1)} %bitcast.6), slice={[0:768], [0:1536]} | slice | bytes 4718592 | tf_op jit(solution)/shard_map/slice | solution.py:288
  2.2 0.8 shard_map.29.turn_ref
  3.0 0.7 collective-permute-start.1
  4.2 1.1 shard_map.30.turn_ref.s_ref
  5.4 1.9 %collective-permute-done.mid_ref = bf16[768,256]{1,0:T(8,128)(2,1)S(1)} collective-permute-done((bf16[768,256]{1,0:T(8,128)(2,1)S(1)}, bf16[768,256]{1,0:T(8,128)(2,1)S(1)}, u32[]{:S(2)}, u32[]{:S(2)}) %collective-permute-start) | collective-permute-done | bytes 393248 | tf_op jit(solution)/shard_map/ppermute | solution.py:293
  7.5 0.7 collective-permute-start.8
  8.1 0.7 collective-permute-start.6
  8.8 0.7 collective-permute-start.7
  9.5 0.7 collective-permute-start.5
  10.2 0.7 collective-permute-start.3
  11.2 0.7 collective-permute-start.10
  11.9 0.7 collective-permute-start.4
  12.5 0.7 collective-permute-start.9
  13.2 0.7 collective-permute-start.12
  14.0 0.7 collective-permute-start.17
  14.7 0.7 collective-permute-start.15
  15.4 0.7 collective-permute-start.14
  16.1 0.7 collective-permute-start.16
  16.8 1.3 %collective-permute-start.11 = (bf16[512,128]{1,0:T(8,128)(2,1)S(1)}, bf16[512,128]{1,0:T(8,128)(2,1)S(1)}, u32[]{:S(2)}, u32[]{:S(2)}) collective-permute-start(bf16[512,128]{1,0:T(8,128)(2,1)S(1)} %get-tuple-element.108), channel_id=1, source_target_pairs={{4,6},{5,7},{18,20},{19,21},{28,30},{29,31}} | collective-permute-start | bytes 393224 | tf_op jit(solution)/shard_map/ppermute | solution.py:328
  18.1 0.7 collective-permute-start.13
  18.8 0.7 collective-permute-start.18
  19.5 0.7 collective-permute-start.19
  20.2 5.9 %collective-permute-done.11.refs_0_.refs_13_ = bf16[512,128]{1,0:T(8,128)(2,1)S(1)} collective-permute-done((bf16[512,128]{1,0:T(8,128)(2,1)S(1)}, bf16[512,128]{1,0:T(8,128)(2,1)S(1)}, u32[]{:S(2)}, u32[]{:S(2)}) %collective-permute-start.11) | collective-permute-done | bytes 131104 | tf_op jit(solution)/shard_map/ppermute | solution.py:328
  26.2 0.7 collective-permute-start.26
  26.9 0.7 collective-permute-start.21
  27.5 0.7 collective-permute-start.24
  28.2 1.3 %collective-permute-start.25 = (bf16[512,128]{1,0:T(8,128)(2,1)S(1)}, bf16[512,128]{1,0:T(8,128)(2,1)S(1)}, u32[]{:S(2)}, u32[]{:S(2)}) collective-permute-start(bf16[512,128]{1,0:T(8,128)(2,1)S(1)} %get-tuple-element.126), channel_id=1, source_target_pairs={{6,8},{7,9},{20,22},{21,23},{28,30},{29,31}} | collective-permute-start | bytes 393224 | tf_op jit(solution)/shard_map/ppermute | solution.py:328
  29.6 0.7 collective-permute-start.23
  30.3 11.2 %collective-permute-done.25.refs_0_.refs_1_.refs_19_ = bf16[512,128]{1,0:T(8,128)(2,1)S(1)} collective-permute-done((bf16[512,128]{1,0:T(8,128)(2,1)S(1)}, bf16[512,128]{1,0:T(8,128)(2,1)S(1)}, u32[]{:S(2)}, u32[]{:S(2)}) %collective-permute-start.25) | collective-permute-done | bytes 131104 | tf_op jit(solution)/shard_map/ppermute | solution.py:328
  42.3 1.3 %collective-permute-start.20 = (bf16[512,128]{1,0:T(8,128)(2,1)S(1)}, bf16[512,128]{1,0:T(8,128)(2,1)S(1)}, u32[]{:S(2)}, u32[]{:S(2)}) collective-permute-start(bf16[512,128]{1,0:T(8,128)(2,1)S(1)} %get-tuple-element.120), channel_id=1, source_target_pairs={{6,8},{7,9},{20,22},{21,23},{28,30},{29,31}} | collective-permute-start | bytes 393224 | tf_op jit(solution)/shard_map/ppermute | solution.py:328
  43.6 1.3 %collective-permute-start.22 = (bf16[512,128]{1,0:T(8,128)(2,1)S(1)}, bf16[512,128]{1,0:T(8,128)(2,1)S(1)}, u32[]{:S(2)}, u32[]{:S(2)}) collective-permute-start(bf16[512,128]{1,0:T(8,128)(2,1)S(1)} %get-tuple-element.123), channel_id=1, source_target_pairs={{6,8},{7,9},{20,22},{21,23},{28,30},{29,31}} | collective-permute-start | bytes 393224 | tf_op jit(solution)/shard_map/ppermute | solution.py:328
  44.9 0.7 collective-permute-start.27
  45.5 2.8 %collective-permute-done.20.refs_0_.refs_18_ = bf16[512,128]{1,0:T(8,128)(2,1)S(1)} collective-permute-done((bf16[512,128]{1,0:T(8,128)(2,1)S(1)}, bf16[512,128]{1,0:T(8,128)(2,1)S(1)}, u32[]{:S(2)}, u32[]{:S(2)}) %collective-permute-start.20) | collective-permute-done | bytes 131104 | tf_op jit(solution)/shard_map/ppermute | solution.py:328
  49.0 0.7 collective-permute-done.22.refs_0_.refs_1_.refs_19_
  49.7 1.5 %slice-done = s8[4194304]{0:T(1024)(128)(4,1)S(1)} async-done(((s8[4718592]{0:T(1024)(128)(4,1)}), s8[4194304]{0:T(1024)(128)(4,1)S(1)}, s32[]{:S(2)}) %slice-start) | async-done | bytes 4194328
  51.5 1.7 %shard_map.63 = (f32[768,1024]{1,0:T(8,128)S(1)}, f32[8,128]{1,0:T(8,128)S(1)}) custom-call(bf16[1536,1536]{1,0:T(8,128)(2,1)S(1)} %bitcast.9, bf16[768,1024]{1,0:T(8,128)(2,1)S(1)} %bitcast.17, bf16[1024,128]{1,0:T(8,128)(2,1)S(1)} %shard_map.62.turn_ref), custom_call_target="tpu_custom_call" | custom-call | tf_op jit(solution)/shard_map/pallas_call | solution.py:347
  53.2 0.7 collective-permute-start.35
  54.0 0.7 collective-permute-start.32
  54.7 0.7 collective-permute-start.33
  55.3 0.7 collective-permute-start.34
  56.0 0.7 collective-permute-start.29
  56.7 0.7 collective-permute-start.31
  57.4 0.7 collective-permute-start.37
  58.2 0.7 collective-permute-start.44
  58.9 0.7 collective-permute-start.36
  59.6 0.7 collective-permute-start.39
  60.3 0.7 collective-permute-start.42
  61.0 0.7 collective-permute-start.43
  62.4 0.7 collective-permute-start.41
  63.2 1.3 %collective-permute-start.45 = (bf16[1024,128]{1,0:T(8,128)(2,1)S(1)}, bf16[1024,128]{1,0:T(8,128)(2,1)S(1)}, u32[]{:S(2)}, u32[]{:S(2)}) collective-permute-start(bf16[1024,128]{1,0:T(8,128)(2,1)S(1)} %shard_map.78.turn_ref), channel_id=1, source_target_pairs={{14,30},{15,31}} | collective-permute-start | bytes 786440 | tf_op jit(solution)/shard_map/ppermute | solution.py:343
  65.1 1.3 %collective-permute-start.46 = (bf16[512,128]{1,0:T(8,128)(2,1)S(1)}, bf16[512,128]{1,0:T(8,128)(2,1)S(1)}, u32[]{:S(2)}, u32[]{:S(2)}) collective-permute-start(bf16[512,128]{1,0:T(8,128)(2,1)S(1)} %get-tuple-element.157), channel_id=1, source_target_pairs={{4,6},{5,7},{18,20},{19,21},{28,30},{29,31}} | collective-permute-start | bytes 393224 | tf_op jit(solution)/shard_map/ppermute | solution.py:328
  66.4 1.3 %collective-permute-start.47 = (bf16[512,128]{1,0:T(8,128)(2,1)S(1)}, bf16[512,128]{1,0:T(8,128)(2,1)S(1)}, u32[]{:S(2)}, u32[]{:S(2)}) collective-permute-start(bf16[512,128]{1,0:T(8,128)(2,1)S(1)} %get-tuple-element.158), channel_id=1, source_target_pairs={{6,8},{7,9},{20,22},{21,23},{28,30},{29,31}} | collective-permute-start | bytes 393224 | tf_op jit(solution)/shard_map/ppermute | solution.py:328
  67.8 19.2 %collective-permute-done.46.refs_38_ = bf16[512,128]{1,0:T(8,128)(2,1)S(1)} collective-permute-done((bf16[512,128]{1,0:T(8,128)(2,1)S(1)}, bf16[512,128]{1,0:T(8,128)(2,1)S(1)}, u32[]{:S(2)}, u32[]{:S(2)}) %collective-permute-start.46) | collective-permute-done | bytes 131104 | tf_op jit(solution)/shard_map/ppermute | solution.py:328
  87.0 1.4 %collective-permute-done.47.refs_39_ = bf16[512,128]{1,0:T(8,128)(2,1)S(1)} collective-permute-done((bf16[512,128]{1,0:T(8,128)(2,1)S(1)}, bf16[512,128]{1,0:T(8,128)(2,1)S(1)}, u32[]{:S(2)}, u32[]{:S(2)}) %collective-permute-start.47) | collective-permute-done | bytes 131104 | tf_op jit(solution)/shard_map/ppermute | solution.py:328
  88.4 5.3 %collective-permute-done.45.refs_37_ = bf16[1024,128]{1,0:T(8,128)(2,1)S(1)} collective-permute-done((bf16[1024,128]{1,0:T(8,128)(2,1)S(1)}, bf16[1024,128]{1,0:T(8,128)(2,1)S(1)}, u32[]{:S(2)}, u32[]{:S(2)}) %collective-permute-start.45) | collective-permute-done | bytes 262176 | tf_op jit(solution)/shard_map/ppermute | solution.py:343
  94.0 12.7 %collective-permute-start.48 = (bf16[768,256]{1,0:T(8,128)(2,1)S(1)}, bf16[768,256]{1,0:T(8,128)(2,1)S(1)}, u32[]{:S(2)}, u32[]{:S(2)}) collective-permute-start(bf16[768,256]{1,0:T(8,128)(2,1)S(1)} %get-tuple-element.159), channel_id=1, source_target_pairs={{0,1},{1,0},{2,3},{3,2},{4,5},{5,4},{6,7},{7,6},{8,9},{9,8},{10,11... | collective-permute-start | bytes 1179656 | tf_op jit(solution)/shard_map/ppermute | solution.py:364
  106.7 1.3 %collective-permute-start.49 = (bf16[1024,128]{1,0:T(8,128)(2,1)S(1)}, bf16[1024,128]{1,0:T(8,128)(2,1)S(1)}, u32[]{:S(2)}, u32[]{:S(2)}) collective-permute-start(bf16[1024,128]{1,0:T(8,128)(2,1)S(1)} %shard_map.81.turn_ref), channel_id=1, source_target_pairs={{14,30},{15,31}} | collective-permute-start | bytes 786440 | tf_op jit(solution)/shard_map/ppermute | solution.py:343
  108.0 1.3 %collective-permute-start.50 = (bf16[512,128]{1,0:T(8,128)(2,1)S(1)}, bf16[512,128]{1,0:T(8,128)(2,1)S(1)}, u32[]{:S(2)}, u32[]{:S(2)}) collective-permute-start(bf16[512,128]{1,0:T(8,128)(2,1)S(1)} %get-tuple-element.163), channel_id=1, source_target_pairs={{6,8},{7,9},{20,22},{21,23},{28,30},{29,31}} | collective-permute-start | bytes 393224 | tf_op jit(solution)/shard_map/ppermute | solution.py:328
  109.3 1.3 %collective-permute-start.51 = (bf16[512,128]{1,0:T(8,128)(2,1)S(1)}, bf16[512,128]{1,0:T(8,128)(2,1)S(1)}, u32[]{:S(2)}, u32[]{:S(2)}) collective-permute-start(bf16[512,128]{1,0:T(8,128)(2,1)S(1)} %get-tuple-element.164), channel_id=1, source_target_pairs={{6,8},{7,9},{20,22},{21,23},{28,30},{29,31}} | collective-permute-start | bytes 393224 | tf_op jit(solution)/shard_map/ppermute | solution.py:328
  111.6 3.3 %collective-permute-done.50.refs_38_ = bf16[512,128]{1,0:T(8,128)(2,1)S(1)} collective-permute-done((bf16[512,128]{1,0:T(8,128)(2,1)S(1)}, bf16[512,128]{1,0:T(8,128)(2,1)S(1)}, u32[]{:S(2)}, u32[]{:S(2)}) %collective-permute-start.50) | collective-permute-done | bytes 131104 | tf_op jit(solution)/shard_map/ppermute | solution.py:328
  114.9 2.8 %collective-permute-done.51.refs_39_ = bf16[512,128]{1,0:T(8,128)(2,1)S(1)} collective-permute-done((bf16[512,128]{1,0:T(8,128)(2,1)S(1)}, bf16[512,128]{1,0:T(8,128)(2,1)S(1)}, u32[]{:S(2)}, u32[]{:S(2)}) %collective-permute-start.51) | collective-permute-done | bytes 131104 | tf_op jit(solution)/shard_map/ppermute | solution.py:328
  118.2 0.9 collective-permute-start.52
  119.5 0.9 collective-permute-done.52.in_ref
  120.4 1.7 %shard_map.87 = bf16[768,1024]{1,0:T(8,128)(2,1)} custom-call(s32[1]{0:T(128)} %bitcast.3.parity_ref, bf16[1536,1536]{1,0:T(8,128)(2,1)S(1)} %bitcast.13, f32[768,1024]{1,0:T(8,128)S(1)} %get-tuple-element.131.r_ref, bf16[768,256]{1,0:T(8,128)(2,1)S(1)} %collective-permute-done.52.in_ref, f32[8,128]{1,0:T(8,128)S(1)} %get-tuple-element.167.turn_ref, ...), custom_call_target="tpu_custom_call" | custom-call | tf_op jit(solution)/shard_map/pallas_call | solution.py:368
  (110 shorter events, 6.7 us)
Async XLA Ops:
  0.0 2.1 %copy-start = (bf16[1,1,1,768,1024]{4,3,2,1,0:T(8,128)(2,1)S(1)}, bf16[1,1,1,768,1024]{4,3,2,1,0:T(8,128)(2,1)}, u32[]{:S(2)}) copy-start(bf16[1,1,1,768,1024]{4,3,2,1,0:T(8,128)(2,1)} %param.3) | copy-start | bytes 4718596
  3.0 4.4 %collective-permute-start.1 = (bf16[768,512]{1,0:T(8,128)(2,1)S(1)}, bf16[768,512]{1,0:T(8,128)(2,1)S(1)}, u32[]{:S(2)}, u32[]{:S(2)}) collective-permute-start(bf16[768,512]{1,0:T(8,128)(2,1)S(1)} %shard_map.29.turn_ref), channel_id=1, source_target_pairs={{0,1},{1,0},{2,3},{3,2},{4,5},{5,4},{6,7},{7,6},{8,9},{9,8},{10,11... | collective-permute-start | bytes 2359304 | tf_op jit(solution)/shard_map/ppermute | solution.py:297
  3.7 6.5 %collective-permute-start.2 = (bf16[768,512]{1,0:T(8,128)(2,1)S(1)}, bf16[768,512]{1,0:T(8,128)(2,1)S(1)}, u32[]{:S(2)}, u32[]{:S(2)}) collective-permute-start(bf16[768,512]{1,0:T(8,128)(2,1)S(1)} %get-tuple-element.98), channel_id=1, source_target_pairs={{0,1},{1,0},{2,3},{3,2},{4,5},{5,4},{6,7},{7,6},{8,9},{9,8},{10,11... | collective-permute-start | bytes 2359304 | tf_op jit(solution)/shard_map/ppermute | solution.py:298
  3.8 3.5 %collective-permute-start = (bf16[768,256]{1,0:T(8,128)(2,1)S(1)}, bf16[768,256]{1,0:T(8,128)(2,1)S(1)}, u32[]{:S(2)}, u32[]{:S(2)}) collective-permute-start(bf16[768,256]{1,0:T(8,128)(2,1)S(1)} %get-tuple-element.93.turn_ref), channel_id=1, source_target_pairs={{0,1},{1,0},{2,3},{3,2},{4,5},{5,4},{6,7},{7,6},{8,9},{9,8},{10,11... | collective-permute-start | bytes 1179656 | tf_op jit(solution)/shard_map/ppermute | solution.py:293
  7.5 3.6 %collective-permute-start.8 = (bf16[1024,128]{1,0:T(8,128)(2,1)S(1)}, bf16[1024,128]{1,0:T(8,128)(2,1)S(1)}, u32[]{:S(2)}, u32[]{:S(2)}) collective-permute-start(bf16[1024,128]{1,0:T(8,128)(2,1)S(1)} %shard_map.34.turn_ref), channel_id=1, source_target_pairs={{0,16},{1,17}} | collective-permute-start | bytes 786440 | tf_op jit(solution)/shard_map/ppermute | solution.py:343
  8.1 3.0 %collective-permute-start.6 = (bf16[512,128]{1,0:T(8,128)(2,1)S(1)}, bf16[512,128]{1,0:T(8,128)(2,1)S(1)}, u32[]{:S(2)}, u32[]{:S(2)}) collective-permute-start(bf16[512,128]{1,0:T(8,128)(2,1)S(1)} %get-tuple-element.101), channel_id=1, source_target_pairs={{0,2},{1,3},{10,12},{11,13},{24,26},{25,27}} | collective-permute-start | bytes 393224 | tf_op jit(solution)/shard_map/ppermute | solution.py:328
  8.8 2.3 %collective-permute-start.7 = (bf16[512,128]{1,0:T(8,128)(2,1)S(1)}, bf16[512,128]{1,0:T(8,128)(2,1)S(1)}, u32[]{:S(2)}, u32[]{:S(2)}) collective-permute-start(bf16[512,128]{1,0:T(8,128)(2,1)S(1)} %get-tuple-element.102), channel_id=1, source_target_pairs={{0,2},{1,3},{8,10},{9,11},{22,24},{23,25}} | collective-permute-start | bytes 393224 | tf_op jit(solution)/shard_map/ppermute | solution.py:328
  9.5 4.4 %collective-permute-start.5 = (bf16[1024,128]{1,0:T(8,128)(2,1)S(1)}, bf16[1024,128]{1,0:T(8,128)(2,1)S(1)}, u32[]{:S(2)}, u32[]{:S(2)}) collective-permute-start(bf16[1024,128]{1,0:T(8,128)(2,1)S(1)} %shard_map.37.turn_ref), channel_id=1, source_target_pairs={{0,16},{1,17}} | collective-permute-start | bytes 786440 | tf_op jit(solution)/shard_map/ppermute | solution.py:343
  10.2 3.0 %collective-permute-start.3 = (bf16[512,128]{1,0:T(8,128)(2,1)S(1)}, bf16[512,128]{1,0:T(8,128)(2,1)S(1)}, u32[]{:S(2)}, u32[]{:S(2)}) collective-permute-start(bf16[512,128]{1,0:T(8,128)(2,1)S(1)} %get-tuple-element.99), channel_id=1, source_target_pairs={{0,2},{1,3},{8,10},{9,11},{22,24},{23,25}} | collective-permute-start | bytes 393224 | tf_op jit(solution)/shard_map/ppermute | solution.py:328
  11.2 4.2 %collective-permute-start.10 = (bf16[1024,128]{1,0:T(8,128)(2,1)S(1)}, bf16[1024,128]{1,0:T(8,128)(2,1)S(1)}, u32[]{:S(2)}, u32[]{:S(2)}) collective-permute-start(bf16[1024,128]{1,0:T(8,128)(2,1)S(1)} %shard_map.41.turn_ref), channel_id=1, source_target_pairs={{2,18},{3,19}} | collective-permute-start | bytes 786440 | tf_op jit(solution)/shard_map/ppermute | solution.py:343
  11.9 2.1 %collective-permute-start.4 = (bf16[512,128]{1,0:T(8,128)(2,1)S(1)}, bf16[512,128]{1,0:T(8,128)(2,1)S(1)}, u32[]{:S(2)}, u32[]{:S(2)}) collective-permute-start(bf16[512,128]{1,0:T(8,128)(2,1)S(1)} %get-tuple-element.100), channel_id=1, source_target_pairs={{0,2},{1,3},{8,10},{9,11},{22,24},{23,25}} | collective-permute-start | bytes 393224 | tf_op jit(solution)/shard_map/ppermute | solution.py:328
  12.5 2.8 %collective-permute-start.9 = (bf16[512,128]{1,0:T(8,128)(2,1)S(1)}, bf16[512,128]{1,0:T(8,128)(2,1)S(1)}, u32[]{:S(2)}, u32[]{:S(2)}) collective-permute-start(bf16[512,128]{1,0:T(8,128)(2,1)S(1)} %get-tuple-element.107), channel_id=1, source_target_pairs={{2,4},{3,5},{12,14},{13,15},{16,18},{17,19},{26,28},{27,29}} | collective-permute-start | bytes 393224 | tf_op jit(solution)/shard_map/ppermute | solution.py:328
  13.2 2.2 %collective-permute-start.12 = (bf16[512,128]{1,0:T(8,128)(2,1)S(1)}, bf16[512,128]{1,0:T(8,128)(2,1)S(1)}, u32[]{:S(2)}, u32[]{:S(2)}) collective-permute-start(bf16[512,128]{1,0:T(8,128)(2,1)S(1)} %get-tuple-element.110), channel_id=1, source_target_pairs={{2,4},{3,5},{10,12},{11,13},{16,18},{17,19},{24,26},{25,27}} | collective-permute-start | bytes 393224 | tf_op jit(solution)/shard_map/ppermute | solution.py:328
  14.0 4.8 %collective-permute-start.17 = (bf16[1024,128]{1,0:T(8,128)(2,1)S(1)}, bf16[1024,128]{1,0:T(8,128)(2,1)S(1)}, u32[]{:S(2)}, u32[]{:S(2)}) collective-permute-start(bf16[1024,128]{1,0:T(8,128)(2,1)S(1)} %shard_map.44.turn_ref), channel_id=1, source_target_pairs={{2,18},{3,19}} | collective-permute-start | bytes 786440 | tf_op jit(solution)/shard_map/ppermute | solution.py:343
  14.7 3.4 %collective-permute-start.15 = (bf16[512,128]{1,0:T(8,128)(2,1)S(1)}, bf16[512,128]{1,0:T(8,128)(2,1)S(1)}, u32[]{:S(2)}, u32[]{:S(2)}) collective-permute-start(bf16[512,128]{1,0:T(8,128)(2,1)S(1)} %get-tuple-element.113), channel_id=1, source_target_pairs={{2,4},{3,5},{10,12},{11,13},{16,18},{17,19},{24,26},{25,27}} | collective-permute-start | bytes 393224 | tf_op jit(solution)/shard_map/ppermute | solution.py:328
  15.4 10.7 %collective-permute-start.14 = (bf16[1024,128]{1,0:T(8,128)(2,1)S(1)}, bf16[1024,128]{1,0:T(8,128)(2,1)S(1)}, u32[]{:S(2)}, u32[]{:S(2)}) collective-permute-start(bf16[1024,128]{1,0:T(8,128)(2,1)S(1)} %shard_map.47.turn_ref), channel_id=1, source_target_pairs={{4,20},{5,21}} | collective-permute-start | bytes 786440 | tf_op jit(solution)/shard_map/ppermute | solution.py:343
  16.1 3.4 %collective-permute-start.16 = (bf16[512,128]{1,0:T(8,128)(2,1)S(1)}, bf16[512,128]{1,0:T(8,128)(2,1)S(1)}, u32[]{:S(2)}, u32[]{:S(2)}) collective-permute-start(bf16[512,128]{1,0:T(8,128)(2,1)S(1)} %get-tuple-element.114), channel_id=1, source_target_pairs={{2,4},{3,5},{10,12},{11,13},{16,18},{17,19},{24,26},{25,27}} | collective-permute-start | bytes 393224 | tf_op jit(solution)/shard_map/ppermute | solution.py:328
  16.8 9.3 %collective-permute-start.11 = (bf16[512,128]{1,0:T(8,128)(2,1)S(1)}, bf16[512,128]{1,0:T(8,128)(2,1)S(1)}, u32[]{:S(2)}, u32[]{:S(2)}) collective-permute-start(bf16[512,128]{1,0:T(8,128)(2,1)S(1)} %get-tuple-element.108), channel_id=1, source_target_pairs={{4,6},{5,7},{18,20},{19,21},{28,30},{29,31}} | collective-permute-start | bytes 393224 | tf_op jit(solution)/shard_map/ppermute | solution.py:328
  18.1 8.0 %collective-permute-start.13 = (bf16[512,128]{1,0:T(8,128)(2,1)S(1)}, bf16[512,128]{1,0:T(8,128)(2,1)S(1)}, u32[]{:S(2)}, u32[]{:S(2)}) collective-permute-start(bf16[512,128]{1,0:T(8,128)(2,1)S(1)} %get-tuple-element.111), channel_id=1, source_target_pairs={{4,6},{5,7},{12,14},{13,15},{18,20},{19,21},{26,28},{27,29}} | collective-permute-start | bytes 393224 | tf_op jit(solution)/shard_map/ppermute | solution.py:328
  18.8 9.4 %collective-permute-start.18 = (bf16[512,128]{1,0:T(8,128)(2,1)S(1)}, bf16[512,128]{1,0:T(8,128)(2,1)S(1)}, u32[]{:S(2)}, u32[]{:S(2)}) collective-permute-start(bf16[512,128]{1,0:T(8,128)(2,1)S(1)} %get-tuple-element.119), channel_id=1, source_target_pairs={{4,6},{5,7},{12,14},{13,15},{18,20},{19,21},{26,28},{27,29}} | collective-permute-start | bytes 393224 | tf_op jit(solution)/shard_map/ppermute | solution.py:328
  19.5 10.0 %collective-permute-start.19 = (bf16[1024,128]{1,0:T(8,128)(2,1)S(1)}, bf16[1024,128]{1,0:T(8,128)(2,1)S(1)}, u32[]{:S(2)}, u32[]{:S(2)}) collective-permute-start(bf16[1024,128]{1,0:T(8,128)(2,1)S(1)} %shard_map.50.turn_ref), channel_id=1, source_target_pairs={{4,20},{5,21}} | collective-permute-start | bytes 786440 | tf_op jit(solution)/shard_map/ppermute | solution.py:343
  26.2 4.1 %collective-permute-start.26 = (bf16[1024,128]{1,0:T(8,128)(2,1)S(1)}, bf16[1024,128]{1,0:T(8,128)(2,1)S(1)}, u32[]{:S(2)}, u32[]{:S(2)}) collective-permute-start(bf16[1024,128]{1,0:T(8,128)(2,1)S(1)} %shard_map.53.turn_ref), channel_id=1, source_target_pairs={{6,22},{7,23}} | collective-permute-start | bytes 786440 | tf_op jit(solution)/shard_map/ppermute | solution.py:343
  26.9 2.7 %collective-permute-start.21 = (bf16[512,128]{1,0:T(8,128)(2,1)S(1)}, bf16[512,128]{1,0:T(8,128)(2,1)S(1)}, u32[]{:S(2)}, u32[]{:S(2)}) collective-permute-start(bf16[512,128]{1,0:T(8,128)(2,1)S(1)} %get-tuple-element.122), channel_id=1, source_target_pairs={{4,6},{5,7},{12,14},{13,15},{18,20},{19,21},{26,28},{27,29}} | collective-permute-start | bytes 393224 | tf_op jit(solution)/shard_map/ppermute | solution.py:328
  27.5 2.8 %collective-permute-start.24 = (bf16[512,128]{1,0:T(8,128)(2,1)S(1)}, bf16[512,128]{1,0:T(8,128)(2,1)S(1)}, u32[]{:S(2)}, u32[]{:S(2)}) collective-permute-start(bf16[512,128]{1,0:T(8,128)(2,1)S(1)} %get-tuple-element.125), channel_id=1, source_target_pairs={{6,8},{7,9},{20,22},{21,23}} | collective-permute-start | bytes 393224 | tf_op jit(solution)/shard_map/ppermute | solution.py:328
  28.2 13.3 %collective-permute-start.25 = (bf16[512,128]{1,0:T(8,128)(2,1)S(1)}, bf16[512,128]{1,0:T(8,128)(2,1)S(1)}, u32[]{:S(2)}, u32[]{:S(2)}) collective-permute-start(bf16[512,128]{1,0:T(8,128)(2,1)S(1)} %get-tuple-element.126), channel_id=1, source_target_pairs={{6,8},{7,9},{20,22},{21,23},{28,30},{29,31}} | collective-permute-start | bytes 393224 | tf_op jit(solution)/shard_map/ppermute | solution.py:328
  29.6 19.4 %collective-permute-start.23 = (bf16[1024,128]{1,0:T(8,128)(2,1)S(1)}, bf16[1024,128]{1,0:T(8,128)(2,1)S(1)}, u32[]{:S(2)}, u32[]{:S(2)}) collective-permute-start(bf16[1024,128]{1,0:T(8,128)(2,1)S(1)} %shard_map.56.turn_ref), channel_id=1, source_target_pairs={{6,22},{7,23}} | collective-permute-start | bytes 786440 | tf_op jit(solution)/shard_map/ppermute | solution.py:343
  41.6 12.3 %collective-permute-start.28 = (bf16[1024,128]{1,0:T(8,128)(2,1)S(1)}, bf16[1024,128]{1,0:T(8,128)(2,1)S(1)}, u32[]{:S(2)}, u32[]{:S(2)}) collective-permute-start(bf16[1024,128]{1,0:T(8,128)(2,1)S(1)} %shard_map.59.turn_ref), channel_id=1, source_target_pairs={{8,24},{9,25}} | collective-permute-start | bytes 786440 | tf_op jit(solution)/shard_map/ppermute | solution.py:343
  42.3 6.1 %collective-permute-start.20 = (bf16[512,128]{1,0:T(8,128)(2,1)S(1)}, bf16[512,128]{1,0:T(8,128)(2,1)S(1)}, u32[]{:S(2)}, u32[]{:S(2)}) collective-permute-start(bf16[512,128]{1,0:T(8,128)(2,1)S(1)} %get-tuple-element.120), channel_id=1, source_target_pairs={{6,8},{7,9},{20,22},{21,23},{28,30},{29,31}} | collective-permute-start | bytes 393224 | tf_op jit(solution)/shard_map/ppermute | solution.py:328
  43.6 6.2 %collective-permute-start.22 = (bf16[512,128]{1,0:T(8,128)(2,1)S(1)}, bf16[512,128]{1,0:T(8,128)(2,1)S(1)}, u32[]{:S(2)}, u32[]{:S(2)}) collective-permute-start(bf16[512,128]{1,0:T(8,128)(2,1)S(1)} %get-tuple-element.123), channel_id=1, source_target_pairs={{6,8},{7,9},{20,22},{21,23},{28,30},{29,31}} | collective-permute-start | bytes 393224 | tf_op jit(solution)/shard_map/ppermute | solution.py:328
  44.9 9.0 %collective-permute-start.27 = (bf16[512,128]{1,0:T(8,128)(2,1)S(1)}, bf16[512,128]{1,0:T(8,128)(2,1)S(1)}, u32[]{:S(2)}, u32[]{:S(2)}) collective-permute-start(bf16[512,128]{1,0:T(8,128)(2,1)S(1)} %get-tuple-element.133), channel_id=1, source_target_pairs={{8,10},{9,11},{22,24},{23,25}} | collective-permute-start | bytes 393224 | tf_op jit(solution)/shard_map/ppermute | solution.py:328
  48.3 5.6 %collective-permute-start.30 = (bf16[512,128]{1,0:T(8,128)(2,1)S(1)}, bf16[512,128]{1,0:T(8,128)(2,1)S(1)}, u32[]{:S(2)}, u32[]{:S(2)}) collective-permute-start(bf16[512,128]{1,0:T(8,128)(2,1)S(1)} %get-tuple-element.136), channel_id=1, source_target_pairs={{0,2},{1,3},{8,10},{9,11},{22,24},{23,25}} | collective-permute-start | bytes 393224 | tf_op jit(solution)/shard_map/ppermute | solution.py:328
  49.0 2.2 %slice-start = ((s8[4718592]{0:T(1024)(128)(4,1)}), s8[4194304]{0:T(1024)(128)(4,1)S(1)}, s32[]{:S(2)}) async-start(s8[4718592]{0:T(1024)(128)(4,1)} %bitcast.7), calls=%async_computation | async-start | bytes 8388608
  49.7 1.7 %slice-start.1 = ((s8[4718592]{0:T(1024)(128)(4,1)}), s8[524288]{0:T(1024)(128)(4,1)S(1)}, s32[]{:S(2)}) async-start(s8[4718592]{0:T(1024)(128)(4,1)} %bitcast.7), calls=%async_computation.1 | async-start | bytes 1048576
  53.2 4.2 %collective-permute-start.35 = (bf16[1024,128]{1,0:T(8,128)(2,1)S(1)}, bf16[1024,128]{1,0:T(8,128)(2,1)S(1)}, u32[]{:S(2)}, u32[]{:S(2)}) collective-permute-start(bf16[1024,128]{1,0:T(8,128)(2,1)S(1)} %shard_map.62.turn_ref), channel_id=1, source_target_pairs={{8,24},{9,25}} | collective-permute-start | bytes 786440 | tf_op jit(solution)/shard_map/ppermute | solution.py:343
  54.0 4.2 %collective-permute-start.32 = (bf16[1024,128]{1,0:T(8,128)(2,1)S(1)}, bf16[1024,128]{1,0:T(8,128)(2,1)S(1)}, u32[]{:S(2)}, u32[]{:S(2)}) collective-permute-start(bf16[1024,128]{1,0:T(8,128)(2,1)S(1)} %shard_map.66.turn_ref), channel_id=1, source_target_pairs={{10,26},{11,27}} | collective-permute-start | bytes 786440 | tf_op jit(solution)/shard_map/ppermute | solution.py:343
  54.7 2.0 %collective-permute-start.33 = (bf16[512,128]{1,0:T(8,128)(2,1)S(1)}, bf16[512,128]{1,0:T(8,128)(2,1)S(1)}, u32[]{:S(2)}, u32[]{:S(2)}) collective-permute-start(bf16[512,128]{1,0:T(8,128)(2,1)S(1)} %get-tuple-element.139), channel_id=1, source_target_pairs={{0,2},{1,3},{8,10},{9,11},{22,24},{23,25}} | collective-permute-start | bytes 393224 | tf_op jit(solution)/shard_map/ppermute | solution.py:328
  55.3 2.1 %collective-permute-start.34 = (bf16[512,128]{1,0:T(8,128)(2,1)S(1)}, bf16[512,128]{1,0:T(8,128)(2,1)S(1)}, u32[]{:S(2)}, u32[]{:S(2)}) collective-permute-start(bf16[512,128]{1,0:T(8,128)(2,1)S(1)} %get-tuple-element.140), channel_id=1, source_target_pairs={{0,2},{1,3},{8,10},{9,11},{22,24},{23,25}} | collective-permute-start | bytes 393224 | tf_op jit(solution)/shard_map/ppermute | solution.py:328
  56.0 2.1 %collective-permute-start.29 = (bf16[512,128]{1,0:T(8,128)(2,1)S(1)}, bf16[512,128]{1,0:T(8,128)(2,1)S(1)}, u32[]{:S(2)}, u32[]{:S(2)}) collective-permute-start(bf16[512,128]{1,0:T(8,128)(2,1)S(1)} %get-tuple-element.134), channel_id=1, source_target_pairs={{0,2},{1,3},{10,12},{11,13},{24,26},{25,27}} | collective-permute-start | bytes 393224 | tf_op jit(solution)/shard_map/ppermute | solution.py:328
  56.7 1.5 %collective-permute-start.31 = (bf16[512,128]{1,0:T(8,128)(2,1)S(1)}, bf16[512,128]{1,0:T(8,128)(2,1)S(1)}, u32[]{:S(2)}, u32[]{:S(2)}) collective-permute-start(bf16[512,128]{1,0:T(8,128)(2,1)S(1)} %get-tuple-element.137), channel_id=1, source_target_pairs={{2,4},{3,5},{10,12},{11,13},{16,18},{17,19},{24,26},{25,27}} | collective-permute-start | bytes 393224 | tf_op jit(solution)/shard_map/ppermute | solution.py:328
  57.4 4.2 %collective-permute-start.37 = (bf16[1024,128]{1,0:T(8,128)(2,1)S(1)}, bf16[1024,128]{1,0:T(8,128)(2,1)S(1)}, u32[]{:S(2)}, u32[]{:S(2)}) collective-permute-start(bf16[1024,128]{1,0:T(8,128)(2,1)S(1)} %shard_map.69.turn_ref), channel_id=1, source_target_pairs={{10,26},{11,27}} | collective-permute-start | bytes 786440 | tf_op jit(solution)/shard_map/ppermute | solution.py:343
  58.2 4.9 %collective-permute-start.44 = (bf16[1024,128]{1,0:T(8,128)(2,1)S(1)}, bf16[1024,128]{1,0:T(8,128)(2,1)S(1)}, u32[]{:S(2)}, u32[]{:S(2)}) collective-permute-start(bf16[1024,128]{1,0:T(8,128)(2,1)S(1)} %shard_map.72.turn_ref), channel_id=1, source_target_pairs={{12,28},{13,29}} | collective-permute-start | bytes 786440 | tf_op jit(solution)/shard_map/ppermute | solution.py:343
  58.9 2.0 %collective-permute-start.36 = (bf16[512,128]{1,0:T(8,128)(2,1)S(1)}, bf16[512,128]{1,0:T(8,128)(2,1)S(1)}, u32[]{:S(2)}, u32[]{:S(2)}) collective-permute-start(bf16[512,128]{1,0:T(8,128)(2,1)S(1)} %get-tuple-element.145), channel_id=1, source_target_pairs={{2,4},{3,5},{10,12},{11,13},{16,18},{17,19},{24,26},{25,27}} | collective-permute-start | bytes 393224 | tf_op jit(solution)/shard_map/ppermute | solution.py:328
  59.6 2.8 %collective-permute-start.39 = (bf16[512,128]{1,0:T(8,128)(2,1)S(1)}, bf16[512,128]{1,0:T(8,128)(2,1)S(1)}, u32[]{:S(2)}, u32[]{:S(2)}) collective-permute-start(bf16[512,128]{1,0:T(8,128)(2,1)S(1)} %get-tuple-element.148), channel_id=1, source_target_pairs={{2,4},{3,5},{10,12},{11,13},{16,18},{17,19},{24,26},{25,27}} | collective-permute-start | bytes 393224 | tf_op jit(solution)/shard_map/ppermute | solution.py:328
  60.3 2.8 %collective-permute-start.42 = (bf16[512,128]{1,0:T(8,128)(2,1)S(1)}, bf16[512,128]{1,0:T(8,128)(2,1)S(1)}, u32[]{:S(2)}, u32[]{:S(2)}) collective-permute-start(bf16[512,128]{1,0:T(8,128)(2,1)S(1)} %get-tuple-element.151), channel_id=1, source_target_pairs={{2,4},{3,5},{12,14},{13,15},{16,18},{17,19},{26,28},{27,29}} | collective-permute-start | bytes 393224 | tf_op jit(solution)/shard_map/ppermute | solution.py:328
  61.0 2.2 %collective-permute-start.43 = (bf16[512,128]{1,0:T(8,128)(2,1)S(1)}, bf16[512,128]{1,0:T(8,128)(2,1)S(1)}, u32[]{:S(2)}, u32[]{:S(2)}) collective-permute-start(bf16[512,128]{1,0:T(8,128)(2,1)S(1)} %get-tuple-element.152), channel_id=1, source_target_pairs={{4,6},{5,7},{12,14},{13,15},{18,20},{19,21},{26,28},{27,29}} | collective-permute-start | bytes 393224 | tf_op jit(solution)/shard_map/ppermute | solution.py:328
  61.7 4.8 %collective-permute-start.38 = (bf16[512,128]{1,0:T(8,128)(2,1)S(1)}, bf16[512,128]{1,0:T(8,128)(2,1)S(1)}, u32[]{:S(2)}, u32[]{:S(2)}) collective-permute-start(bf16[512,128]{1,0:T(8,128)(2,1)S(1)} %get-tuple-element.146), channel_id=1, source_target_pairs={{4,6},{5,7},{12,14},{13,15},{18,20},{19,21},{26,28},{27,29}} | collective-permute-start | bytes 393224 | tf_op jit(solution)/shard_map/ppermute | solution.py:328
  62.4 5.4 %collective-permute-start.41 = (bf16[1024,128]{1,0:T(8,128)(2,1)S(1)}, bf16[1024,128]{1,0:T(8,128)(2,1)S(1)}, u32[]{:S(2)}, u32[]{:S(2)}) collective-permute-start(bf16[1024,128]{1,0:T(8,128)(2,1)S(1)} %shard_map.75.turn_ref), channel_id=1, source_target_pairs={{12,28},{13,29}} | collective-permute-start | bytes 786440 | tf_op jit(solution)/shard_map/ppermute | solution.py:343
  63.2 30.5 %collective-permute-start.45 = (bf16[1024,128]{1,0:T(8,128)(2,1)S(1)}, bf16[1024,128]{1,0:T(8,128)(2,1)S(1)}, u32[]{:S(2)}, u32[]{:S(2)}) collective-permute-start(bf16[1024,128]{1,0:T(8,128)(2,1)S(1)} %shard_map.78.turn_ref), channel_id=1, source_target_pairs={{14,30},{15,31}} | collective-permute-start | bytes 786440 | tf_op jit(solution)/shard_map/ppermute | solution.py:343
  64.5 3.3 %collective-permute-start.40 = (bf16[512,128]{1,0:T(8,128)(2,1)S(1)}, bf16[512,128]{1,0:T(8,128)(2,1)S(1)}, u32[]{:S(2)}, u32[]{:S(2)}) collective-permute-start(bf16[512,128]{1,0:T(8,128)(2,1)S(1)} %get-tuple-element.149), channel_id=1, source_target_pairs={{4,6},{5,7},{12,14},{13,15},{18,20},{19,21},{26,28},{27,29}} | collective-permute-start | bytes 393224 | tf_op jit(solution)/shard_map/ppermute | solution.py:328
  65.1 21.9 %collective-permute-start.46 = (bf16[512,128]{1,0:T(8,128)(2,1)S(1)}, bf16[512,128]{1,0:T(8,128)(2,1)S(1)}, u32[]{:S(2)}, u32[]{:S(2)}) collective-permute-start(bf16[512,128]{1,0:T(8,128)(2,1)S(1)} %get-tuple-element.157), channel_id=1, source_target_pairs={{4,6},{5,7},{18,20},{19,21},{28,30},{29,31}} | collective-permute-start | bytes 393224 | tf_op jit(solution)/shard_map/ppermute | solution.py:328
  66.4 22.0 %collective-permute-start.47 = (bf16[512,128]{1,0:T(8,128)(2,1)S(1)}, bf16[512,128]{1,0:T(8,128)(2,1)S(1)}, u32[]{:S(2)}, u32[]{:S(2)}) collective-permute-start(bf16[512,128]{1,0:T(8,128)(2,1)S(1)} %get-tuple-element.158), channel_id=1, source_target_pairs={{6,8},{7,9},{20,22},{21,23},{28,30},{29,31}} | collective-permute-start | bytes 393224 | tf_op jit(solution)/shard_map/ppermute | solution.py:328
  94.0 17.1 %collective-permute-start.48 = (bf16[768,256]{1,0:T(8,128)(2,1)S(1)}, bf16[768,256]{1,0:T(8,128)(2,1)S(1)}, u32[]{:S(2)}, u32[]{:S(2)}) collective-permute-start(bf16[768,256]{1,0:T(8,128)(2,1)S(1)} %get-tuple-element.159), channel_id=1, source_target_pairs={{0,1},{1,0},{2,3},{3,2},{4,5},{5,4},{6,7},{7,6},{8,9},{9,8},{10,11... | collective-permute-start | bytes 1179656 | tf_op jit(solution)/shard_map/ppermute | solution.py:364
  106.7 11.1 %collective-permute-start.49 = (bf16[1024,128]{1,0:T(8,128)(2,1)S(1)}, bf16[1024,128]{1,0:T(8,128)(2,1)S(1)}, u32[]{:S(2)}, u32[]{:S(2)}) collective-permute-start(bf16[1024,128]{1,0:T(8,128)(2,1)S(1)} %shard_map.81.turn_ref), channel_id=1, source_target_pairs={{14,30},{15,31}} | collective-permute-start | bytes 786440 | tf_op jit(solution)/shard_map/ppermute | solution.py:343
  108.0 6.9 %collective-permute-start.50 = (bf16[512,128]{1,0:T(8,128)(2,1)S(1)}, bf16[512,128]{1,0:T(8,128)(2,1)S(1)}, u32[]{:S(2)}, u32[]{:S(2)}) collective-permute-start(bf16[512,128]{1,0:T(8,128)(2,1)S(1)} %get-tuple-element.163), channel_id=1, source_target_pairs={{6,8},{7,9},{20,22},{21,23},{28,30},{29,31}} | collective-permute-start | bytes 393224 | tf_op jit(solution)/shard_map/ppermute | solution.py:328
  109.3 8.4 %collective-permute-start.51 = (bf16[512,128]{1,0:T(8,128)(2,1)S(1)}, bf16[512,128]{1,0:T(8,128)(2,1)S(1)}, u32[]{:S(2)}, u32[]{:S(2)}) collective-permute-start(bf16[512,128]{1,0:T(8,128)(2,1)S(1)} %get-tuple-element.164), channel_id=1, source_target_pairs={{6,8},{7,9},{20,22},{21,23},{28,30},{29,31}} | collective-permute-start | bytes 393224 | tf_op jit(solution)/shard_map/ppermute | solution.py:328
  118.2 2.2 %collective-permute-start.52 = (bf16[768,256]{1,0:T(8,128)(2,1)S(1)}, bf16[768,256]{1,0:T(8,128)(2,1)S(1)}, u32[]{:S(2)}, u32[]{:S(2)}) collective-permute-start(bf16[768,256]{1,0:T(8,128)(2,1)S(1)} %get-tuple-element.165), channel_id=1, source_target_pairs={{0,1},{1,0},{2,3},{3,2},{4,5},{5,4},{6,7},{7,6},{8,9},{9,8},{10,11... | collective-permute-start | bytes 1179656 | tf_op jit(solution)/shard_map/ppermute | solution.py:364
